TPU v7x, 32 devices: a whole 2x2x4 slice. The times are simulated.
32 devices in a mesh: mc: 4 (over z), space: 8 (over y, x, core).
Axes of the slice: x: 2, y: 2, z: 4, core: 2. Of those that a mesh axis runs over, the one named last changes fastest.
Arguments:
- orbit_state: float32 [6, 1048576], P(None, ('mc', 'space')), parts along dimension 1, may hold values from -1.3 to 1.3, as said below
- object_props: float32 [3, 1048576], P(None, ('mc', 'space')), parts along dimension 1, may hold values from 0.5 to 2
- density_table: float32 [64], replicated, may hold values from -1 to 1
- block_cube: int32 [8192], P(('mc', 'space')), parts along dimension 0, may hold values from 0 to 1023, as said below
Outputs:
- next_state: float32 [6, 1048576], P(None, ('mc', 'space')), parts along dimension 1
- collision_rate: float32 [1048576], P(('mc', 'space')), parts along dimension 0
There are 4 independent parts, one for each index of `mc`. A program takes and returns all parts, laid end to end along the dimension named above; an argument that names none is the same for every part. Nothing has to cross between parts.
Inputs may be any that keep to these rules, and one draw needn't show every extreme that they name: `orbit_state`: rows 0 to 2 are a position with 1.08 <= |r| <= 1.3, rows 3 to 5 a velocity of speed between 0.86 and 0.98. `block_cube`: cube c is owned by the device of index c // 128 along space. No cube holds more than 4 blocks in all, and in every draw some cube holds exactly 4. The blocks of one device include at most 64 whose cubes have any one owner, and in every draw some owner receives exactly 64 blocks from every device.
All inputs are finite; a program needn't handle non-finite values.
Results may differ from a plain program's by a relative error of at most 0.0003.
Values sent between devices are 32-bit elements; how exact they have to be, the bound alone decides.
No kernel may reach another device: no remote copies, remote signals or barrier semaphores. Data moves between devices by JAX's collectives and lax.ppermute only.
A program may use at most 64 MiB of HBM per device.

v0:
```python
import math

import jax
import jax.numpy as jnp
from jax import lax
from jax.sharding import PartitionSpec as P

BLK = 128
MOST = 4
SUB = 16
NTAB = 64


TIME_STEP = 0.2
EARTH_SPIN = 0.0588
J2_COEF = 0.00108263
DRAG_SCALE = 0.008
SCALE_HEIGHT = 0.1
TABLE_TOP = 0.4
SPEED_FLOOR = 0.04


def propagate(orbit_part, prop_part, density_table):
    position = orbit_part[0:3]
    velocity = orbit_part[3:6]
    ballistic = prop_part[2]
    alt_grid = jnp.arange(NTAB).astype(density_table.dtype)
    for substep in range(SUB):
        radius_sq = jnp.sum(position * position, axis=0)
        radius = jnp.sqrt(radius_sq)
        height = radius - 1.0
        table_coord = height * ((NTAB - 1) / TABLE_TOP)
        hat_weights = jnp.maximum(0.0, 1.0 - jnp.abs(table_coord[None, :] - alt_grid[:, None]))
        log_density = (
            jnp.dot(density_table[None, :], hat_weights, precision=lax.Precision.HIGHEST)[0]
            - height / SCALE_HEIGHT
        )
        density = DRAG_SCALE * jnp.exp(log_density)
        relative = jnp.stack(
            [
                velocity[0] + EARTH_SPIN * position[1],
                velocity[1] - EARTH_SPIN * position[0],
                velocity[2],
            ]
        )
        air_speed = jnp.sqrt(jnp.sum(relative * relative, axis=0))
        inv_cube = 1.0 / (radius_sq * radius)
        polar_ratio = position[2] * position[2] / radius_sq
        oblate_factor = 1.5 * J2_COEF / (radius_sq * radius_sq * radius)
        shape_term = jnp.stack(
            [1.0 - 5.0 * polar_ratio, 1.0 - 5.0 * polar_ratio, 3.0 - 5.0 * polar_ratio]
        )
        acceleration = (
            -position * inv_cube
            - oblate_factor * position * shape_term
            - density * ballistic * air_speed * relative
        )
        velocity = velocity + TIME_STEP * acceleration
        position = position + TIME_STEP * velocity
    return jnp.concatenate([position, velocity], axis=0)


def propagate_all(orbit_state, object_props, density_table):
    total_count = orbit_state.shape[1]
    span_width = math.gcd(total_count, 4096)
    groups = total_count // span_width
    stacked = orbit_state.reshape(6, groups, span_width).transpose(1, 0, 2)
    prop_stack = object_props.reshape(3, groups, span_width).transpose(1, 0, 2)
    advanced = lax.map(
        lambda packed: propagate(packed[0], packed[1], density_table), (stacked, prop_stack)
    )
    return advanced.transpose(1, 0, 2).reshape(6, total_count)


def tile_rates(own_rows, mate_rows, column_ok, self_column):
    group_size = own_rows.shape[1]
    span_width = mate_rows.shape[2]
    diff_sq = jnp.zeros((group_size, BLK, span_width), own_rows.dtype)
    for component in range(3):
        velocity_gap = own_rows[component][:, :, None] - mate_rows[component][:, None, :]
        diff_sq = diff_sq + velocity_gap * velocity_gap
    same_index = (jnp.arange(BLK)[:, None] == (jnp.arange(span_width) % BLK)[None, :])[None, :, :]
    keep_mask = column_ok[:, None, :] & jnp.logical_not(self_column[:, None, :] & same_index)
    pair_term = jnp.where(
        keep_mask,
        mate_rows[4][:, None, :]
        * (own_rows[3][:, :, None] + mate_rows[3][:, None, :]) ** 2
        * jnp.sqrt(diff_sq + SPEED_FLOOR),
        0.0,
    )
    return own_rows[4] * jnp.sum(pair_term, axis=2) / span_width


def find_partners(cube_value):
    slot_count = cube_value.shape[0]
    slot_index = jnp.arange(slot_count)
    live_slot = cube_value >= 0.0
    same_cube = (cube_value[:, None] == cube_value[None, :]) & live_slot[:, None]
    scores = jnp.where(
        same_cube, 2 * slot_count - slot_index[None, :], slot_count - slot_index[None, :]
    )
    values, partners = lax.top_k(scores, MOST)
    return (partners, values > slot_count)


def holder_groups(own_all, held_rows, held_code):
    block_count = own_all.shape[1]
    group_size = math.gcd(block_count, 32)

    def one_group(first_block):
        own_rows = lax.dynamic_slice_in_dim(own_all, first_block, group_size, 1)
        mate_rows = lax.dynamic_slice_in_dim(held_rows, first_block, group_size, 1).reshape(
            5, group_size, MOST * BLK
        )
        code_rows = lax.dynamic_slice_in_dim(held_code, first_block, group_size, 0)
        column_ok = jnp.repeat(code_rows > 0.5, BLK, axis=1)
        self_column = jnp.repeat(code_rows > 1.5, BLK, axis=1)
        return tile_rates(own_rows, mate_rows, column_ok, self_column)

    block_rates = lax.map(one_group, jnp.arange(0, block_count, group_size))
    return block_rates.reshape(block_count, BLK)


def on_device(orbit_state, object_props, density_table, block_cube):
    space_size = lax.axis_size("space")
    block_count = block_cube.shape[0]
    object_count = orbit_state.shape[1]
    next_state = propagate_all(orbit_state, object_props, density_table)
    capacity = (2 * block_count + space_size - 1) // space_size
    slot_count = space_size * capacity
    cubes_owned = slot_count // MOST
    block_owner = block_cube // cubes_owned
    onehot = (block_owner[:, None] == jnp.arange(space_size)[None, :]).astype(jnp.int32)
    slot_rank = jnp.sum((jnp.cumsum(onehot, axis=0) - onehot) * onehot, axis=1)
    block_slot = block_owner * capacity + slot_rank
    matches = block_slot[None, :] == jnp.arange(slot_count)[:, None]
    filled = jnp.any(matches, axis=1)
    source = jnp.sum(jnp.where(matches, jnp.arange(block_count)[None, :], 0), axis=1)
    cube_out = jnp.where(filled, jnp.take(block_cube, source), -1).astype(jnp.float32)[None, :]
    records = jnp.concatenate([next_state[3:6], object_props[0:2]], axis=0)
    own_all = records.reshape(5, block_count, BLK)
    outgoing = jnp.where(filled[None, :, None], jnp.take(own_all, source, axis=1), 0.0)
    received, cube_in = (
        lax.all_to_all(outgoing, "space", split_axis=1, concat_axis=1, tiled=True),
        lax.all_to_all(cube_out, "space", split_axis=1, concat_axis=1, tiled=True),
    )
    partners, partner_ok = find_partners(cube_in[0])
    slot_index = jnp.arange(slot_count)
    partner_rows = jnp.take(received, partners, axis=1)
    mate_code = jnp.where(
        partner_ok, jnp.where(partners == slot_index[:, None], 2.0, 1.0), 0.0
    ).astype(jnp.float32)[None]
    rows_back, code_back = (
        lax.all_to_all(partner_rows, "space", split_axis=1, concat_axis=1, tiled=True),
        lax.all_to_all(mate_code, "space", split_axis=1, concat_axis=1, tiled=True),
    )
    held_rows = jnp.take(rows_back, block_slot, axis=1)
    held_code = jnp.take(code_back[0], block_slot, axis=0)
    own_rates = holder_groups(own_all, held_rows, held_code).reshape(object_count)
    return (next_state, own_rates)


def solution(mesh):
    placed = (P(None, ("mc", "space")), P(None, ("mc", "space")), P(), P(("mc", "space")))
    return jax.shard_map(
        on_device,
        mesh=mesh,
        in_specs=placed,
        out_specs=(P(None, ("mc", "space")), P(("mc", "space"))),
        check_vma=False,
    )
```

profile of v0, /device:TPU:0, one launch (start us, length us, event | category | flops | bytes accessed | tf_op | source)
XLA Modules:
  0.0 501.4 jit_solution(5412980219766728963)
XLA Ops:
  10.7 3.6 gather_fusion
  15.1 5.2 %all-to-all-start = ((f32[1,8,64]{2,0,1:T(1,128)}), f32[1,8,64]{2,0,1:T(1,128)S(1)}, u32[]{:S(2)}, u32[]{:S(2)}) async-start(f32[1,8,64]{2,0,1:T(1,128)} %bitcast.75), calls=%async_computation | async-start | bytes 8192 | tf_op jit(solution)/shard_map/all_to_all | solution.py:145
  20.3 4.5 all-to-all-done
  28.5 200.8 %while.25 = (s32[]{:T(128)}, f32[8,6,4096]{2,1,0:T(8,128)S(1)}, f32[8,6,4096]{2,1,0:T(8,128)}, f32[64]{0:T(128)S(1)}, f32[8,3,4096]{2,1,0:T(4,128)S(1)}, /*index...) while((s32[]{:T(128)}, f32[8,6,4096]{2,1,0:T(8,128)S(1)}, f32[8,6,4096]{2,1,0:T(8,128)}, ...), condition=%wide.region_33.34_spmd, body=%wide.region_0.33_spmd.sunk | while | flops 72573000 | bytes 13459949 | solution.py:69
  28.8 1.4 fusion.530
  78.9 1.3 fusion.530
  103.9 1.3 fusion.530
  129.0 1.3 fusion.530
  154.0 1.4 fusion.530
  230.5 1.9 gather_fusion.2
  232.4 3.4 select_bitcast_fusion.1
  235.8 3.6 all-to-all-start.2
  241.0 2.0 reduce.6
  243.0 1.7 reshape.1186
  246.9 19.0 %all-to-all-done.2 = f32[5,512,128]{2,0,1:T(8,128)S(1)} async-done(((f32[5,512,128]{2,0,1:T(8,128)}), f32[5,512,128]{2,0,1:T(8,128)S(1)}, u32[]{:S(2)}, u32[]{:S(2)}) %all-to-all-start.2) | async-done | bytes 1310752 | tf_op jit(solution)/shard_map/all_to_all | solution.py:144
  265.9 3.3 all-to-all-start.1
  269.3 17.7 %gather_fusion.3 = f32[2048,5,128]{2,1,0:T(8,128)} fusion(f32[5,512,128]{2,0,1:T(8,128)S(1)} %all-to-all-done.2, s32[2048]{0:T(1024)S(1)} %broadcast_clamp_fusion), kind=kCustom, calls=%fused_computation.3 | custom fusion | bytes 10493952 | tf_op jit(solution)/shard_map/jit(_take)/gather | solution.py:149
  286.9 8.7 %fusion.377 = f32[5,512,4,128]{3,2,0,1:T(4,128)} fusion(f32[512,4,5,128]{3,2,1,0:T(8,128)} %bitcast.340, pred[512,4]{1,0:T(8,128)(4,1)S(1)} %compare_and_fusion), kind=kLoop, calls=%fused_computation.636 | loop fusion | flops 1310720 | bytes 10487808 | tf_op jit(solution)/shard_map/jit(_take)/select_n | solution.py:149
  295.6 4.6 all-to-all-start.3
  302.3 58.2 %all-to-all-done.3 = f32[5,512,4,128]{3,2,0,1:T(4,128)} async-done(((f32[5,512,4,128]{3,2,0,1:T(4,128)}), f32[5,512,4,128]{3,2,0,1:T(4,128)}, u32[]{:S(2)}, u32[]{:S(2)}) %all-to-all-start.3) | async-done | bytes 5242912 | tf_op jit(solution)/shard_map/all_to_all | solution.py:154
  360.6 5.7 %copy.33 = f32[5,512,4,128]{3,2,1,0:T(4,128)} copy(f32[5,512,4,128]{3,2,0,1:T(4,128)} %all-to-all-done.3) | data formatting | bytes 10485760 | tf_op jit(solution)/shard_map/all_to_all | solution.py:154
  366.3 5.1 %gather_fusion.4 = f32[256,5,4,128]{3,2,1,0:T(4,128)S(1)} fusion(f32[5,512,4,128]{3,2,1,0:T(4,128)} %copy.33, s32[1024]{0:T(1024)S(1)} %pad_clamp_fusion), kind=kCustom, calls=%fused_computation.4 | custom fusion | bytes 5243904 | tf_op jit(solution)/shard_map/jit(_take)/gather | solution.py:157
  371.4 2.2 select_bitcast_fusion
  373.6 120.9 %while.26 = (s32[]{:T(128)}, f32[8,32,128]{2,1,0:T(8,128)}, s32[8]{0:T(128)S(1)}, f32[5,256,128]{2,1,0:T(8,128)S(1)}, f32[256,4]{1,0:T(8,128)S(1)}, /*index=5*/f...) while((s32[]{:T(128)}, f32[8,32,128]{2,1,0:T(8,128)}, ...), condition=%wide.region_42.43_spmd, body=%wide.region_40.42_spmd.sunk | while | flops 37821704 | bytes 2168087 | solution.py:120
  377.5 10.6 %select_reduce_fusion.3 = f32[32,128]{1,0:T(8,128)S(1)} fusion(f32[32,512]{1,0:T(8,128)S(1)} %get-tuple-element.904, f32[32,128]{1,0:T(8,128)S(1)} %get-tuple-element.905, f32[32,512]{1,0:T(8,128)S(1)} %get-tuple-element.906, f32[32,128]{1,0:T(8,128)S(1)} %get-tuple-element.907, f32[32,512]{1,0:T(8,128)S(1)} %get-tuple-element.910, ...), kind=kLoop, calls=%fused_computation.607.clone.1 | loop fusion | flops 37744640 | bytes 507904 | tf_op jit(solution)/shard_map/while/body/eval_jaxpr/reduce_sum | solution.py:91
  392.6 10.6 %select_reduce_fusion.3 = f32[32,128]{1,0:T(8,128)S(1)} fusion(f32[32,512]{1,0:T(8,128)S(1)} %get-tuple-element.904, f32[32,128]{1,0:T(8,128)S(1)} %get-tuple-element.905, f32[32,512]{1,0:T(8,128)S(1)} %get-tuple-element.906, f32[32,128]{1,0:T(8,128)S(1)} %get-tuple-element.907, f32[32,512]{1,0:T(8,128)S(1)} %get-tuple-element.910, ...), kind=kLoop, calls=%fused_computation.607.clone.1 | loop fusion | flops 37744640 | bytes 507904 | tf_op jit(solution)/shard_map/while/body/eval_jaxpr/reduce_sum | solution.py:91
  407.7 10.6 %select_reduce_fusion.3 = f32[32,128]{1,0:T(8,128)S(1)} fusion(f32[32,512]{1,0:T(8,128)S(1)} %get-tuple-element.904, f32[32,128]{1,0:T(8,128)S(1)} %get-tuple-element.905, f32[32,512]{1,0:T(8,128)S(1)} %get-tuple-element.906, f32[32,128]{1,0:T(8,128)S(1)} %get-tuple-element.907, f32[32,512]{1,0:T(8,128)S(1)} %get-tuple-element.910, ...), kind=kLoop, calls=%fused_computation.607.clone.1 | loop fusion | flops 37744640 | bytes 507904 | tf_op jit(solution)/shard_map/while/body/eval_jaxpr/reduce_sum | solution.py:91
  422.8 10.6 %select_reduce_fusion.3 = f32[32,128]{1,0:T(8,128)S(1)} fusion(f32[32,512]{1,0:T(8,128)S(1)} %get-tuple-element.904, f32[32,128]{1,0:T(8,128)S(1)} %get-tuple-element.905, f32[32,512]{1,0:T(8,128)S(1)} %get-tuple-element.906, f32[32,128]{1,0:T(8,128)S(1)} %get-tuple-element.907, f32[32,512]{1,0:T(8,128)S(1)} %get-tuple-element.910, ...), kind=kLoop, calls=%fused_computation.607.clone.1 | loop fusion | flops 37744640 | bytes 507904 | tf_op jit(solution)/shard_map/while/body/eval_jaxpr/reduce_sum | solution.py:91
  438.0 10.6 %select_reduce_fusion.3 = f32[32,128]{1,0:T(8,128)S(1)} fusion(f32[32,512]{1,0:T(8,128)S(1)} %get-tuple-element.904, f32[32,128]{1,0:T(8,128)S(1)} %get-tuple-element.905, f32[32,512]{1,0:T(8,128)S(1)} %get-tuple-element.906, f32[32,128]{1,0:T(8,128)S(1)} %get-tuple-element.907, f32[32,512]{1,0:T(8,128)S(1)} %get-tuple-element.910, ...), kind=kLoop, calls=%fused_computation.607.clone.1 | loop fusion | flops 37744640 | bytes 507904 | tf_op jit(solution)/shard_map/while/body/eval_jaxpr/reduce_sum | solution.py:91
  453.1 10.6 %select_reduce_fusion.3 = f32[32,128]{1,0:T(8,128)S(1)} fusion(f32[32,512]{1,0:T(8,128)S(1)} %get-tuple-element.904, f32[32,128]{1,0:T(8,128)S(1)} %get-tuple-element.905, f32[32,512]{1,0:T(8,128)S(1)} %get-tuple-element.906, f32[32,128]{1,0:T(8,128)S(1)} %get-tuple-element.907, f32[32,512]{1,0:T(8,128)S(1)} %get-tuple-element.910, ...), kind=kLoop, calls=%fused_computation.607.clone.1 | loop fusion | flops 37744640 | bytes 507904 | tf_op jit(solution)/shard_map/while/body/eval_jaxpr/reduce_sum | solution.py:91
  468.2 10.6 %select_reduce_fusion.3 = f32[32,128]{1,0:T(8,128)S(1)} fusion(f32[32,512]{1,0:T(8,128)S(1)} %get-tuple-element.904, f32[32,128]{1,0:T(8,128)S(1)} %get-tuple-element.905, f32[32,512]{1,0:T(8,128)S(1)} %get-tuple-element.906, f32[32,128]{1,0:T(8,128)S(1)} %get-tuple-element.907, f32[32,512]{1,0:T(8,128)S(1)} %get-tuple-element.910, ...), kind=kLoop, calls=%fused_computation.607.clone.1 | loop fusion | flops 37744640 | bytes 507904 | tf_op jit(solution)/shard_map/while/body/eval_jaxpr/reduce_sum | solution.py:91
  483.3 10.6 %select_reduce_fusion.3 = f32[32,128]{1,0:T(8,128)S(1)} fusion(f32[32,512]{1,0:T(8,128)S(1)} %get-tuple-element.904, f32[32,128]{1,0:T(8,128)S(1)} %get-tuple-element.905, f32[32,512]{1,0:T(8,128)S(1)} %get-tuple-element.906, f32[32,128]{1,0:T(8,128)S(1)} %get-tuple-element.907, f32[32,512]{1,0:T(8,128)S(1)} %get-tuple-element.910, ...), kind=kLoop, calls=%fused_computation.607.clone.1 | loop fusion | flops 37744640 | bytes 507904 | tf_op jit(solution)/shard_map/while/body/eval_jaxpr/reduce_sum | solution.py:91
  (1081 shorter events, 222.9 us)
Async XLA Ops:
  7.2 21.4 %copy-start.1 = (f32[3,32768]{1,0:T(4,128)S(1)}, f32[3,32768]{1,0:T(4,128)}, u32[]{:S(2)}) copy-start(f32[3,32768]{1,0:T(4,128)} %param.9) | copy-start | bytes 1179652
  7.2 21.4 %copy-start.2 = (f32[64]{0:T(128)S(1)}, f32[64]{0:T(128)}, u32[]{:S(2)}) copy-start(f32[64]{0:T(128)} %param.10) | copy-start | bytes 772
  15.1 9.8 %all-to-all-start = ((f32[1,8,64]{2,0,1:T(1,128)}), f32[1,8,64]{2,0,1:T(1,128)S(1)}, u32[]{:S(2)}, u32[]{:S(2)}) async-start(f32[1,8,64]{2,0,1:T(1,128)} %bitcast.75), calls=%async_computation | async-start | bytes 8192 | tf_op jit(solution)/shard_map/all_to_all | solution.py:145
  20.3 219.1 %top_k.29.cloned.1.call-start = ((), (), s32[]{:S(2)}) async-start(), calls=%async_computation.4 | async-start | bytes 6291488 | tf_op jit(solution)/shard_map/top_k | solution.py:102
  229.3 1.0 copy-start
  235.8 30.2 %all-to-all-start.2 = ((f32[5,512,128]{2,0,1:T(8,128)}), f32[5,512,128]{2,0,1:T(8,128)S(1)}, u32[]{:S(2)}, u32[]{:S(2)}) async-start(f32[5,512,128]{2,0,1:T(8,128)} %select_bitcast_fusion.1), calls=%async_computation.2 | async-start | bytes 4194304 | tf_op jit(solution)/shard_map/all_to_all | solution.py:144
  265.9 29.7 %all-to-all-start.1 = ((f32[8,1,256]{2,1,0:T(1,128)}), f32[8,1,256]{2,1,0:T(1,128)S(1)}, u32[]{:S(2)}, u32[]{:S(2)}) async-start(f32[8,1,256]{2,1,0:T(1,128)} %reshape.1186), calls=%async_computation.1 | async-start | bytes 16384 | tf_op jit(solution)/shard_map/all_to_all | solution.py:155
  295.6 65.0 %all-to-all-start.3 = ((f32[5,512,4,128]{3,2,0,1:T(4,128)}), f32[5,512,4,128]{3,2,0,1:T(4,128)}, u32[]{:S(2)}, u32[]{:S(2)}) async-start(f32[5,512,4,128]{3,2,0,1:T(4,128)} %fusion.377), calls=%async_computation.3 | async-start | bytes 10485760 | tf_op jit(solution)/shard_map/all_to_all | solution.py:154
Sparse Core Ops, SparseCore 0:
  28.7 38.1 top_k.31.cloned.1.call-done
  (1 shorter events, 0.0 us)
where the time goes:
time: 503 us; the launch traced here: 501 us
  other arithmetic  202 us (40%)
  matrix products  109 us (22%)
  waiting for transfers between devices  81.8 us (16%)
  local copies, waits for them, and re-layouts  56 us (11%)
  loops' own time  22.1 us (4%)
  starting transfers between devices  16.8 us (3%)
  between operations  14.3 us (3%)
    dot_general x128, matrix products, propagate(): jnp.dot(density_table[None, :], hat_weights, precision=lax.Precision.HIGH...  109 us
    reduce_sum x8, other arithmetic, tile_rates(): return own_rows[4] * jnp.sum(pair_term, axis=2) / span_width  85 us
    all_to_all x1, waiting for transfers between devices, on_device(): lax.all_to_all(partner_rows, 'space', split_axis=1, concat_axis=1, tiled=...  58.2 us
    reduce_sum x120, other arithmetic, propagate(): radius_sq = jnp.sum(position * position, axis=0)  28.8 us
    sub x128, other arithmetic, propagate(): 1.0 - 5.0 * polar_ratio  19 us
    all_to_all x1, waiting for transfers between devices, on_device(): lax.all_to_all(outgoing, 'space', split_axis=1, concat_axis=1, tiled=True)  19 us
    reduce_sum x128, other arithmetic, propagate(): air_speed = jnp.sqrt(jnp.sum(relative * relative, axis=0))  18.5 us
    gather x1, local copies, waits for them, and re-layouts, on_device(): partner_rows = jnp.take(received, partners, axis=1)  17.7 us
  transfers between devices with their start and end apart: 4, of which 3 were waited for; matrix products, arithmetic and copies ran while one was open for 7% of the time, Pallas kernels for 0%

commit v1 on v0

v1 whole, which is shorter than its diff:
```python
import functools

import jax
import jax.numpy as jnp
from jax import lax
from jax.experimental import pallas as pl
from jax.experimental.pallas import tpu as pltpu
from jax.sharding import PartitionSpec as P

LANES = 128
MOST = 4
SUB = 16
NTAB = 64

TIME_STEP = 0.2
EARTH_SPIN = 0.0588
J2_COEF = 0.00108263
DRAG_SCALE = 0.008
SCALE_HEIGHT = 0.1
TABLE_TOP = 0.4
SPEED_FLOOR = 0.04

F32 = jnp.float32
BF = jnp.bfloat16


def substep(state, ballistic, table, slopes):
    x, y, z, vx, vy, vz = state
    zz = z * z
    radius_sq = x * x + y * y + zz
    inv = lax.rsqrt(radius_sq)
    height = radius_sq * inv - 1.0
    coord = jnp.clip(height * ((NTAB - 1) / TABLE_TOP), -1.0, float(NTAB))
    cell = jnp.floor(coord)
    index = cell.astype(jnp.int32) + 1
    base = jnp.take_along_axis(table, index, axis=1, mode="promise_in_bounds")
    slope = jnp.take_along_axis(slopes, index, axis=1, mode="promise_in_bounds")
    log_density = base + (coord - cell) * slope - height * (1.0 / SCALE_HEIGHT)
    ux = vx + EARTH_SPIN * y
    uy = vy - EARTH_SPIN * x
    air_sq = ux * ux + uy * uy + vz * vz
    drag = (TIME_STEP * DRAG_SCALE) * jnp.exp(log_density) * (ballistic * jnp.sqrt(air_sq))
    inv_sq = inv * inv
    inv_cube = inv_sq * inv
    oblate = (1.5 * J2_COEF * TIME_STEP) * (inv_cube * inv_sq)
    pull = TIME_STEP * inv_cube + oblate * (1.0 - 5.0 * (zz * inv_sq))
    pull_z = pull + 2.0 * oblate
    vx = vx - x * pull - drag * ux
    vy = vy - y * pull - drag * uy
    vz = vz - z * pull_z - drag * vz
    return (x + TIME_STEP * vx, y + TIME_STEP * vy, z + TIME_STEP * vz, vx, vy, vz)


def propagate_kernel(table_ref, orbit_ref, props_ref, next_ref, vel_a, vel_b, tiles, drags, *, group, unroll):
    blocks = orbit_ref.shape[1] // LANES
    half = blocks // 2
    for b in range(blocks):
        tiles[pl.ds(8 * b, 6), :] = orbit_ref[:, pl.ds(b * LANES, LANES)]
        drags[pl.ds(8 * b, 1), :] = props_ref[pl.ds(2, 1), pl.ds(b * LANES, LANES)]
    rows = group * 8
    table = jnp.broadcast_to(table_ref[pl.ds(0, 1), :], (rows, LANES))
    slopes = jnp.broadcast_to(table_ref[pl.ds(1, 1), :], (rows, LANES))

    def chunk(i, start, out_ref):
        base = pl.multiple_of((start + i * rows) * 8, 8 * rows)
        state = tuple(tiles[pl.ds(base + c, rows, stride=8), :] for c in range(6))
        ballistic = drags[pl.ds(base, rows, stride=8), :]
        state = lax.fori_loop(
            0, SUB, lambda k, s: substep(s, ballistic, table, slopes), state, unroll=unroll
        )
        for c in range(6):
            tiles[pl.ds(base + c, rows, stride=8), :] = state[c]
        for c in range(3):
            out_ref[pl.ds(pl.multiple_of(c * half + i * rows, 8), rows), :] = state[3 + c]

    for start, out_ref in ((0, vel_a), (half, vel_b)):
        for i in range(half // rows):
            chunk(i, start, out_ref)
    for b in range(blocks):
        next_ref[:, pl.ds(b * LANES, LANES)] = tiles[pl.ds(8 * b, 6), :]


def propagate(table, orbit_state, object_props):
    count = orbit_state.shape[1]
    blocks = count // LANES
    vel = jax.ShapeDtypeStruct((3 * blocks // 2, LANES), F32)
    return pl.pallas_call(
        functools.partial(propagate_kernel, group=16, unroll=2),
        out_shape=(jax.ShapeDtypeStruct((6, count), F32), vel, vel),
        scratch_shapes=[pltpu.VMEM((blocks * 8, LANES), F32), pltpu.VMEM((blocks * 8, LANES), F32)],
        name="propagate",
    )(table, orbit_state, object_props)


def split3(a):
    high = a.astype(BF).astype(F32)
    rest = a - high
    mid = rest.astype(BF).astype(F32)
    return high, mid, rest - mid


def rates_kernel(order_ref, parts_ref, most_ref, *refs, pieces, half, srows, group):
    s_in = refs[: 2 * pieces]
    v_in = refs[2 * pieces : 4 * pieces]
    out_ref, gs, gv, lhs_ref, cols, sem = refs[4 * pieces :]
    blocks = 2 * half
    vrows = 3 * half
    copies = []
    row_s = row_v = 0
    for a, b in zip(s_in, v_in):
        copies.append(pltpu.make_async_copy(a, gs.at[pl.ds(row_s, a.shape[0]), :], sem.at[len(copies)]))
        copies.append(pltpu.make_async_copy(b, gv.at[pl.ds(row_v, b.shape[0]), :], sem.at[len(copies)]))
        row_s += a.shape[0]
        row_v += b.shape[0]
    for c in copies:
        c.start()
    gs[pl.ds(row_s, srows), :] = jnp.zeros((srows, LANES), F32)
    gv[pl.ds(row_v, vrows), :] = jnp.zeros((vrows, LANES), F32)
    for c in copies:
        c.wait()
    units = row_s // srows // 2
    sub = lax.broadcasted_iota(jnp.int32, (8, LANES), 0)
    lane = lax.broadcasted_iota(jnp.int32, (LANES, LANES), 1)
    one = jnp.ones((8, LANES), F32)

    def pick(rows):
        out = rows[7]
        for k in range(6, -1, -1):
            out = jnp.where(sub == k, rows[k], out)
        return out

    def load(ref, r):
        return jnp.broadcast_to(ref[pl.ds(r, 1), :], (8, LANES))

    def own_features(b, carry):
        u = (b // half) * units
        r = b % half
        vx, vy, vz = (load(gv, u * vrows + c * half + r) for c in range(3))
        rad = load(gs, u * srows + r)
        speed_sq = vx * vx + vy * vy + vz * vz
        own = pick([-2.0 * vx, -2.0 * vy, -2.0 * vz, one, speed_sq, rad * rad, 2.0 * rad, one])
        high, mid, low = split3(own)
        rows = jnp.concatenate([high, high, mid, mid, high, low, jnp.zeros((80, LANES), F32)], 0)
        lhs_ref[pl.ds(pl.multiple_of(b * LANES, LANES), LANES), :] = rows.T.astype(BF)
        return carry

    lax.fori_loop(0, blocks, own_features, 0, unroll=2)
    pad = jnp.zeros((80, LANES), BF)

    def mate_features(p):
        u = p // half
        r = p % half
        vx, vy, vz = (load(gv, u * vrows + c * half + r) for c in range(3))
        rad = load(gs, u * srows + r)
        wt = load(gs, u * srows + half + r)
        wr = wt * rad
        speed_sq = vx * vx + vy * vy + vz * vz
        mate = pick([vx, vy, vz, speed_sq + SPEED_FLOOR, one, wt, wr, wr * rad])
        out = []
        for keep in (sub < 5, sub >= 5):
            high, mid, low = split3(jnp.where(keep, mate, 0.0))
            top = jnp.concatenate([high, mid], 0).astype(BF)
            bottom = jnp.concatenate([low, high], 0).astype(BF)
            out.append(jnp.concatenate([top, top, bottom, pad], 0))
        return out

    def run(g, count):
        for k in range(group):
            slot = g * group + k
            b = order_ref[slot]
            lhs = lhs_ref[pl.ds(pl.multiple_of(b * LANES, LANES), LANES), :]
            acc = None
            for p in range(count):
                gap_rows, size_rows = mate_features(parts_ref[slot * MOST + p])
                gap = jnp.dot(lhs, gap_rows, preferred_element_type=F32)
                size = jnp.dot(lhs, size_rows, preferred_element_type=F32)
                gap = jnp.maximum(gap, SPEED_FLOOR)
                term = size * (gap * lax.rsqrt(gap))
                acc = term if acc is None else acc + term
            col = jnp.sum(acc, axis=1, keepdims=True)
            tile = b // LANES
            at = pl.ds(pl.multiple_of(tile * LANES, LANES), LANES)
            cols[at, :] = jnp.where(lane == b - tile * LANES, col, cols[at, :])

    def step(g, carry):
        most = most_ref[g]
        for count in range(1, MOST + 1):

            @pl.when(most == count)
            def _():
                run(g, count)

        return carry

    lax.fori_loop(0, blocks // group, step, 0)
    for b in range(0, blocks, LANES):
        total = cols[pl.ds(b, LANES), :].T
        at = (b // half) * units * srows + b % half
        rad = gs[pl.ds(at, LANES), :]
        wt = gs[pl.ds(at + half, LANES), :]
        self_term = (4.0 * SPEED_FLOOR**0.5) * wt * rad * rad
        out_ref[pl.ds(b, LANES), :] = wt * (total - self_term) * (1.0 / (MOST * LANES))


def rates(order, parts, most, s_pieces, v_pieces, half, srows, group):
    pieces = len(s_pieces) // 2
    total_s = sum(a.shape[0] for a in s_pieces) + srows
    total_v = sum(a.shape[0] for a in v_pieces) + 3 * half
    return pl.pallas_call(
        functools.partial(rates_kernel, pieces=pieces, half=half, srows=srows, group=group),
        in_specs=[pl.BlockSpec(memory_space=pltpu.SMEM)] * 3
        + [pl.BlockSpec(memory_space=pl.ANY)] * (4 * pieces),
        out_shape=jax.ShapeDtypeStruct((2 * half, LANES), F32),
        scratch_shapes=[
            pltpu.VMEM((total_s, LANES), F32),
            pltpu.VMEM((total_v, LANES), F32),
            pltpu.VMEM((2 * half * LANES, LANES), BF),
            pltpu.VMEM((2 * half, LANES), F32),
            pltpu.SemaphoreType.DMA((4 * pieces,)),
        ],
        name="rates",
    )(order, parts, most, *s_pieces, *v_pieces)


def find_partners(own, every, group):
    blocks = own.shape[0]
    total = every.shape[0]
    index = jnp.arange(total, dtype=jnp.int32)[None, :]
    same = own[:, None] == every[None, :]
    last = jnp.full((blocks,), -1, jnp.int32)
    found = []
    for _ in range(MOST):
        last = jnp.min(jnp.where(same & (index > last[:, None]), index, total), axis=1)
        found.append(last)
    parts = jnp.stack(found, 1)
    count = jnp.sum((parts < total).astype(jnp.int32), axis=1)
    ids = jnp.arange(blocks, dtype=jnp.int32)
    ahead = (count[None, :] > count[:, None]) | (
        (count[None, :] == count[:, None]) & (ids[None, :] < ids[:, None])
    )
    rank = jnp.sum(ahead.astype(jnp.int32), axis=1)
    at_slot = (rank[None, :] == ids[:, None]).astype(jnp.int32)
    order = jnp.sum(at_slot * ids[None, :], axis=1)
    parts = jnp.sum(at_slot[:, :, None] * parts[None], axis=1)
    most = jnp.sum(at_slot * count[None, :], axis=1)[::group]
    return order, parts.reshape(-1), most


def exchange(own_a, own_b, size):
    bits = [1 << k for k in range(size.bit_length() - 2, -1, -1)]
    swapped = bits[1::-1] + bits[2:]

    def send(a, bit):
        return lax.ppermute(a, "space", [(i, i ^ bit) for i in range(size)])

    pieces_a, pieces_b = [own_a], [own_b]
    for bit_a, bit_b in zip(bits, swapped):
        out_a = jnp.concatenate(pieces_a, 0) if len(pieces_a) > 1 else own_a
        out_b = jnp.concatenate(pieces_b, 0) if len(pieces_b) > 1 else own_b
        pieces_a.append(send(out_a, bit_a))
        pieces_b.append(send(out_b, bit_b))
    return pieces_a, pieces_b


def on_device(orbit_state, object_props, density_table, block_cube):
    size = lax.axis_size("space")
    blocks = block_cube.shape[0]
    half = blocks // 2
    group = 8
    table = jnp.pad(density_table, (1, LANES - NTAB - 1))
    table = jnp.stack([table, jnp.pad(density_table, (0, LANES - NTAB)) - table])
    cube_rows = -(-half // (8 * LANES)) * 8
    srows = 2 * half + cube_rows
    planes = object_props[0:2].reshape(2, blocks, LANES)
    cubes = block_cube.astype(F32)

    def static(lo):
        ids = jnp.pad(cubes[lo : lo + half], (0, cube_rows * LANES - half))
        rows = planes[:, lo : lo + half].reshape(2 * half, LANES)
        return jnp.concatenate([rows, ids.reshape(cube_rows, LANES)], 0)

    s_a, s_b = exchange(static(0), static(half), size)
    every = jnp.concatenate(
        [a.reshape(-1, srows, LANES)[:, 2 * half :].reshape(-1, cube_rows * LANES)[:, :half] for a in s_a + s_b]
    ).reshape(-1)
    next_state, vel_a, vel_b = propagate(table, orbit_state, object_props)
    v_a, v_b = exchange(vel_a, vel_b, size)
    order, parts, most = find_partners(cubes, every, group)
    out = rates(order, parts, most, s_a + s_b, v_a + v_b, half, srows, group)
    return (next_state, out.reshape(blocks * LANES))


def solution(mesh):
    placed = (P(None, ("mc", "space")), P(None, ("mc", "space")), P(), P(("mc", "space")))
    return jax.shard_map(
        on_device,
        mesh=mesh,
        in_specs=placed,
        out_specs=(P(None, ("mc", "space")), P(("mc", "space"))),
        check_vma=False,
    )
```

time: 503 us -> 88.2 us (0.18)
  other arithmetic: 202 us -> 5.3 us
  matrix products: 109 us -> 0 us
  waiting for transfers between devices: 81.8 us -> 13.8 us
  Pallas kernels: 0 us -> 50.4 us
  local copies, waits for them, and re-layouts: 56 us -> 6.12 us
  loops' own time: 22.1 us -> 0 us
  between operations: 14.3 us -> 0.95 us
  starting transfers between devices: 16.8 us -> 11.1 us
    reduce_sum x258 -> x4, other arithmetic: 132 us -> 1.16 us  [the longest x1 0.73 us: find_partners(): most = jnp.sum(at_slot * count[None, :], axis=1)[::group]]
    dot_general x128 -> x0, matrix products: 109 us -> none  [propagate(): jnp.dot(density_table[None, :], hat_weights, precision=lax.Precision.HIGH...]
    all_to_all x4 -> x0, waiting for transfers between devices: 81.8 us -> none  [the longest x1 58.2 us: on_device(): lax.all_to_all(partner_rows, 'space', split_axis=1, concat_axis=1, tiled=...]
    pallas_call x0 -> x2, Pallas kernels: none -> 50.4 us  [the longest x1 40.9 us: rates(): pl.pallas_call(functools.partial(rates_kernel, pieces=pieces, half=half,...]
    gather x6 -> x0, local copies, waits for them, and re-layouts: 29.1 us -> none  [the longest x1 17.7 us: on_device(): partner_rows = jnp.take(received, partners, axis=1)]
    another operation x2 -> x0, loops' own time: 22.1 us -> none  [the longest x1 15.6 us: holder_groups(): block_rates = lax.map(one_group, jnp.arange(0, block_count, group_size))]
    sub x257 -> x0, other arithmetic: 21.1 us -> none  [the longest x128 19 us: propagate(): 1.0 - 5.0 * polar_ratio]
    select_n x18 -> x0, other arithmetic: 18.4 us -> none  [the longest x2 9.66 us: on_device(): partner_rows = jnp.take(received, partners, axis=1)]
  transfers between devices with their start and end apart: 4 -> 12, of which waited for: 3 -> 4; matrix products, arithmetic and copies ran while one was open for 7% -> 7% of each run, Pallas kernels for 0% -> 11%
where the time goes in v1:
time: 88.2 us; the launch traced here: 87.6 us
  Pallas kernels  50.4 us (57%)
  waiting for transfers between devices  13.8 us (16%)
  starting transfers between devices  11.1 us (13%)
  local copies, waits for them, and re-layouts  6.12 us (7%)
  other arithmetic  5.3 us (6%)
  between operations  0.95 us (1%)
    pallas_call x1, Pallas kernels, rates(): pl.pallas_call(functools.partial(rates_kernel, pieces=pieces, half=half,...  40.9 us
    ppermute x12, waiting for transfers between devices, send(): return lax.ppermute(a, 'space', [(i, i ^ bit) for i in range(size)])  13.8 us
    ppermute x12, starting transfers between devices, send(): return lax.ppermute(a, 'space', [(i, i ^ bit) for i in range(size)])  11.1 us
    pallas_call x1, Pallas kernels, propagate(): pl.pallas_call(functools.partial(propagate_kernel, group=16, unroll=2), o...  9.51 us
    unnamed x42, local copies, waits for them, and re-layouts  4.46 us
    reduce_min x4, other arithmetic, find_partners(): jnp.min(jnp.where(same & (index > last[:, None]), index, total), axis=1)  2.47 us
  transfers between devices with their start and end apart: 12, of which 4 were waited for; matrix products, arithmetic and copies ran while one was open for 7% of the time, Pallas kernels for 11%

profile of v1, /device:TPU:0, one launch (start us, length us, event | category | flops | bytes accessed | tf_op | source)
XLA Modules:
  0.0 87.6 jit_solution(3242771354150733459)
XLA Ops:
  0.6 0.7 convert_element_type.23
  1.3 1.1 %slice_bitcast_fusion = f32[1,2,256,128]{3,1,2,0:T(2,128)S(1)} fusion(f32[3,32768]{1,0:T(4,128)} %props_ref.1), kind=kLoop, calls=%fused_computation.27 | loop fusion | bytes 524288
  2.6 3.1 %collective-permute-start = (f32[264,128]{1,0:T(8,128)S(1)}, f32[264,128]{1,0:T(8,128)S(1)}, u32[]{:S(2)}, u32[]{:S(2)}) collective-permute-start(f32[264,128]{1,0:T(8,128)S(1)} %get-tuple-element.16.refs_0_), channel_id=1, source_target_pairs={{0,4},{1,5},{2,6},{3,7},{4,0},{5,1},{6,2},{7,3},{8,12},{9,13},{10,... | collective-permute-start | bytes 405512 | tf_op jit(solution)/shard_map/ppermute | solution.py:254
  5.7 1.6 %collective-permute-start.3 = (f32[264,128]{1,0:T(8,128)S(1)}, f32[264,128]{1,0:T(8,128)S(1)}, u32[]{:S(2)}, u32[]{:S(2)}) collective-permute-start(f32[264,128]{1,0:T(8,128)S(1)} %get-tuple-element.14.refs_4_), channel_id=1, source_target_pairs={{0,2},{1,3},{2,0},{3,1},{4,6},{5,7},{6,4},{7,5},{8,10},{9,11},{10,... | collective-permute-start | bytes 405512 | tf_op jit(solution)/shard_map/ppermute | solution.py:254
  7.3 0.6 pad_maximum_fusion.10.table_ref
  7.9 9.5 %propagate.1 = (f32[6,32768]{1,0:T(8,128)}, f32[384,128]{1,0:T(8,128)}, f32[384,128]{1,0:T(8,128)}) custom-call(f32[2,128]{1,0:T(2,128)} %pad_maximum_fusion.10.table_ref, f32[6,32768]{1,0:T(8,128)} %orbit_ref.1, f32[3,32768]{1,0:T(4,128)} %props_ref.1), custom_call_target="tpu_custom_call" | custom-call | tf_op jit(solution)/shard_map/propagate/pallas_call | solution.py:87
  17.4 0.5 collective-permute-start.6
  17.9 0.1 collective-permute-start.9
  18.1 2.0 %collective-permute-start.4 = (f32[528,128]{1,0:T(8,128)S(1)}, f32[528,128]{1,0:T(8,128)S(1)}, u32[]{:S(2)}, u32[]{:S(2)}) collective-permute-start(f32[528,128]{1,0:T(8,128)S(1)} %pad_maximum_fusion.7), channel_id=1, source_target_pairs={{0,4},{1,5},{2,6},{3,7},{4,0},{5,1},{6,2},{7,3},{8,12},{9,13},{10,... | collective-permute-start | bytes 811016 | tf_op jit(solution)/shard_map/ppermute | solution.py:254
  20.2 1.6 %collective-permute-start.1 = (f32[528,128]{1,0:T(8,128)S(1)}, f32[528,128]{1,0:T(8,128)S(1)}, u32[]{:S(2)}, u32[]{:S(2)}) collective-permute-start(f32[528,128]{1,0:T(8,128)S(1)} %pad_maximum_fusion.6), channel_id=1, source_target_pairs={{0,2},{1,3},{2,0},{3,1},{4,6},{5,7},{6,4},{7,5},{8,10},{9,11},{10,... | collective-permute-start | bytes 811016 | tf_op jit(solution)/shard_map/ppermute | solution.py:254
  21.7 3.6 %collective-permute-done.6.refs_9_ = f32[384,128]{1,0:T(8,128)S(1)} collective-permute-done((f32[384,128]{1,0:T(8,128)}, f32[384,128]{1,0:T(8,128)S(1)}, u32[]{:S(2)}, u32[]{:S(2)}) %collective-permute-start.6) | collective-permute-done | bytes 196640 | tf_op jit(solution)/shard_map/ppermute | solution.py:254
  25.4 0.6 collective-permute-start.7
  26.1 1.5 %collective-permute-start.10 = (f32[768,128]{1,0:T(8,128)S(1)}, f32[768,128]{1,0:T(8,128)S(1)}, u32[]{:S(2)}, u32[]{:S(2)}) collective-permute-start(f32[768,128]{1,0:T(8,128)S(1)} %pad_maximum_fusion.5), channel_id=1, source_target_pairs={{0,4},{1,5},{2,6},{3,7},{4,0},{5,1},{6,2},{7,3},{8,12},{9,13},{10,... | collective-permute-start | bytes 1179656 | tf_op jit(solution)/shard_map/ppermute | solution.py:254
  27.5 3.7 %collective-permute-done.4.refs_6_ = f32[528,128]{1,0:T(8,128)S(1)} collective-permute-done((f32[528,128]{1,0:T(8,128)S(1)}, f32[528,128]{1,0:T(8,128)S(1)}, u32[]{:S(2)}, u32[]{:S(2)}) %collective-permute-start.4) | collective-permute-done | bytes 270368 | tf_op jit(solution)/shard_map/ppermute | solution.py:254
  31.3 0.4 collective-permute-done.1.refs_2_
  31.7 0.2 copy-done.8
  32.0 6.1 %collective-permute-done.7.refs_10_ = f32[768,128]{1,0:T(8,128)S(1)} collective-permute-done((f32[768,128]{1,0:T(8,128)S(1)}, f32[768,128]{1,0:T(8,128)S(1)}, u32[]{:S(2)}, u32[]{:S(2)}) %collective-permute-start.7) | collective-permute-done | bytes 393248 | tf_op jit(solution)/shard_map/ppermute | solution.py:254
  38.4 0.5 copy-done.4
  38.9 0.8 copy-done.11
  39.8 0.8 copy-done.12
  40.6 0.7 select_reduce_fusion.3
  41.3 0.6 select_reduce_fusion.2
  41.9 0.6 select_reduce_fusion.1
  42.5 0.6 select_reduce_fusion
  43.1 0.2 convert_reduce_fusion
  43.3 0.7 select_reduce_fusion.4
  44.0 0.7 slice.87.most_ref
  44.8 0.2 multiply_reduce_fusion
  45.0 0.1 copy.7
  45.1 0.7 reshape.120.parts_ref
  45.9 0.9 %copy-done.10 = f32[1536,128]{1,0:T(8,128)} copy-done((f32[1536,128]{1,0:T(8,128)}, f32[1536,128]{1,0:T(8,128)S(1)}, u32[]{:S(2)}) %copy-start.10) | copy-done | bytes 786456
  46.8 40.9 %rates.1 = f32[256,128]{1,0:T(8,128)} custom-call(s32[256]{0:T(256)} %get-tuple-element.9.order_ref, s32[1024]{0:T(1024)} %reshape.120.parts_ref, s32[32]{0:T(128)} %slice.87.most_ref, f32[264,128]{1,0:T(8,128)} %copy-done.13, f32[264,128]{1,0:T(8,128)} %copy-done.6, f32[528,128]{1,0:T(8,128)} %copy-done.9, f32[1056,128]{1,0:T(8,128)} %copy-done.12, ...), custom_call_target="tpu_custom_call" | custom-call | tf_op jit(solution)/shard_map/rates/pallas_call | solution.py:209
  (79 shorter events, 0.9 us)
Async XLA Ops:
  2.5 4.8 %copy-start.15 = (f32[64]{0:T(128)S(1)}, f32[64]{0:T(128)}, u32[]{:S(2)}) copy-start(f32[64]{0:T(128)} %param.6) | copy-start | bytes 772
  2.6 15.5 %copy-start.13 = (f32[264,128]{1,0:T(8,128)}, f32[264,128]{1,0:T(8,128)S(1)}, u32[]{:S(2)}) copy-start(f32[264,128]{1,0:T(8,128)S(1)} %get-tuple-element.16.refs_0_) | copy-start | bytes 405508
  2.6 17.5 %collective-permute-start = (f32[264,128]{1,0:T(8,128)S(1)}, f32[264,128]{1,0:T(8,128)S(1)}, u32[]{:S(2)}, u32[]{:S(2)}) collective-permute-start(f32[264,128]{1,0:T(8,128)S(1)} %get-tuple-element.16.refs_0_), channel_id=1, source_target_pairs={{0,4},{1,5},{2,6},{3,7},{4,0},{5,1},{6,2},{7,3},{8,12},{9,13},{10,... | collective-permute-start | bytes 405512 | tf_op jit(solution)/shard_map/ppermute | solution.py:254
  5.7 12.4 %copy-start.14 = (f32[264,128]{1,0:T(8,128)}, f32[264,128]{1,0:T(8,128)S(1)}, u32[]{:S(2)}) copy-start(f32[264,128]{1,0:T(8,128)S(1)} %get-tuple-element.14.refs_4_) | copy-start | bytes 405508
  5.7 12.4 %collective-permute-start.3 = (f32[264,128]{1,0:T(8,128)S(1)}, f32[264,128]{1,0:T(8,128)S(1)}, u32[]{:S(2)}, u32[]{:S(2)}) collective-permute-start(f32[264,128]{1,0:T(8,128)S(1)} %get-tuple-element.14.refs_4_), channel_id=1, source_target_pairs={{0,2},{1,3},{2,0},{3,1},{4,6},{5,7},{6,4},{7,5},{8,10},{9,11},{10,... | collective-permute-start | bytes 405512 | tf_op jit(solution)/shard_map/ppermute | solution.py:254
  17.4 8.0 %copy-start = (f32[384,128]{1,0:T(8,128)S(1)}, f32[384,128]{1,0:T(8,128)}, u32[]{:S(2)}) copy-start(f32[384,128]{1,0:T(8,128)} %get-tuple-element.6.refs_8_) | copy-start | bytes 589828
  17.4 8.6 %copy-start.1 = (f32[384,128]{1,0:T(8,128)S(1)}, f32[384,128]{1,0:T(8,128)}, u32[]{:S(2)}) copy-start(f32[384,128]{1,0:T(8,128)} %get-tuple-element.7.refs_12_) | copy-start | bytes 589828
  17.4 8.0 %collective-permute-start.6 = (f32[384,128]{1,0:T(8,128)}, f32[384,128]{1,0:T(8,128)S(1)}, u32[]{:S(2)}, u32[]{:S(2)}) collective-permute-start(f32[384,128]{1,0:T(8,128)} %get-tuple-element.6.refs_8_), channel_id=1, source_target_pairs={{0,4},{1,5},{2,6},{3,7},{4,0},{5,1},{6,2},{7,3},{8,12},{9,13},{10,... | collective-permute-start | bytes 589832 | tf_op jit(solution)/shard_map/ppermute | solution.py:254
  17.9 8.1 %collective-permute-start.9 = (f32[384,128]{1,0:T(8,128)}, f32[384,128]{1,0:T(8,128)S(1)}, u32[]{:S(2)}, u32[]{:S(2)}) collective-permute-start(f32[384,128]{1,0:T(8,128)} %get-tuple-element.7.refs_12_), channel_id=1, source_target_pairs={{0,2},{1,3},{2,0},{3,1},{4,6},{5,7},{6,4},{7,5},{8,10},{9,11},{10,... | collective-permute-start | bytes 589832 | tf_op jit(solution)/shard_map/ppermute | solution.py:254
  18.0 13.1 %copy-start.7 = (f32[264,128]{1,0:T(8,128)}, f32[264,128]{1,0:T(8,128)S(1)}, u32[]{:S(2)}) copy-start(f32[264,128]{1,0:T(8,128)S(1)} %collective-permute-done.3.refs_5_) | copy-start | bytes 405508
  18.1 13.1 %collective-permute-start.4 = (f32[528,128]{1,0:T(8,128)S(1)}, f32[528,128]{1,0:T(8,128)S(1)}, u32[]{:S(2)}, u32[]{:S(2)}) collective-permute-start(f32[528,128]{1,0:T(8,128)S(1)} %pad_maximum_fusion.7), channel_id=1, source_target_pairs={{0,4},{1,5},{2,6},{3,7},{4,0},{5,1},{6,2},{7,3},{8,12},{9,13},{10,... | collective-permute-start | bytes 811016 | tf_op jit(solution)/shard_map/ppermute | solution.py:254
  20.1 11.6 %copy-start.6 = (f32[264,128]{1,0:T(8,128)}, f32[264,128]{1,0:T(8,128)S(1)}, u32[]{:S(2)}) copy-start(f32[264,128]{1,0:T(8,128)S(1)} %collective-permute-done.refs_1_) | copy-start | bytes 405508
  20.2 11.5 %collective-permute-start.1 = (f32[528,128]{1,0:T(8,128)S(1)}, f32[528,128]{1,0:T(8,128)S(1)}, u32[]{:S(2)}, u32[]{:S(2)}) collective-permute-start(f32[528,128]{1,0:T(8,128)S(1)} %pad_maximum_fusion.6), channel_id=1, source_target_pairs={{0,2},{1,3},{2,0},{3,1},{4,6},{5,7},{6,4},{7,5},{8,10},{9,11},{10,... | collective-permute-start | bytes 811016 | tf_op jit(solution)/shard_map/ppermute | solution.py:254
  25.4 12.8 %copy-start.2 = (f32[384,128]{1,0:T(8,128)}, f32[384,128]{1,0:T(8,128)S(1)}, u32[]{:S(2)}) copy-start(f32[384,128]{1,0:T(8,128)S(1)} %collective-permute-done.6.refs_9_) | copy-start | bytes 589828
  25.4 12.7 %collective-permute-start.7 = (f32[768,128]{1,0:T(8,128)S(1)}, f32[768,128]{1,0:T(8,128)S(1)}, u32[]{:S(2)}, u32[]{:S(2)}) collective-permute-start(f32[768,128]{1,0:T(8,128)S(1)} %pad_maximum_fusion.4), channel_id=1, source_target_pairs={{0,2},{1,3},{2,0},{3,1},{4,6},{5,7},{6,4},{7,5},{8,10},{9,11},{10,... | collective-permute-start | bytes 1179656 | tf_op jit(solution)/shard_map/ppermute | solution.py:254
  26.0 12.3 %copy-start.3 = (f32[384,128]{1,0:T(8,128)}, f32[384,128]{1,0:T(8,128)S(1)}, u32[]{:S(2)}) copy-start(f32[384,128]{1,0:T(8,128)S(1)} %collective-permute-done.9.refs_13_) | copy-start | bytes 589828
  26.1 12.2 %collective-permute-start.10 = (f32[768,128]{1,0:T(8,128)S(1)}, f32[768,128]{1,0:T(8,128)S(1)}, u32[]{:S(2)}, u32[]{:S(2)}) collective-permute-start(f32[768,128]{1,0:T(8,128)S(1)} %pad_maximum_fusion.5), channel_id=1, source_target_pairs={{0,4},{1,5},{2,6},{3,7},{4,0},{5,1},{6,2},{7,3},{8,12},{9,13},{10,... | collective-permute-start | bytes 1179656 | tf_op jit(solution)/shard_map/ppermute | solution.py:254
  31.2 0.7 copy-start.8
  31.2 7.7 %collective-permute-start.5 = (f32[1056,128]{1,0:T(8,128)S(1)}, f32[1056,128]{1,0:T(8,128)S(1)}, u32[]{:S(2)}, u32[]{:S(2)}) collective-permute-start(f32[1056,128]{1,0:T(8,128)S(1)} %pad_maximum_fusion.3), channel_id=1, source_target_pairs={{0,1},{1,0},{2,3},{3,2},{4,5},{5,4},{6,7},{7,6},{8,9},{9,8},{10,11... | collective-permute-start | bytes 1622024 | tf_op jit(solution)/shard_map/ppermute | solution.py:254
  31.7 6.5 %copy-start.9 = (f32[528,128]{1,0:T(8,128)}, f32[528,128]{1,0:T(8,128)S(1)}, u32[]{:S(2)}) copy-start(f32[528,128]{1,0:T(8,128)S(1)} %collective-permute-done.1.refs_2_) | copy-start | bytes 811012
  31.9 7.8 %collective-permute-start.2 = (f32[1056,128]{1,0:T(8,128)S(1)}, f32[1056,128]{1,0:T(8,128)S(1)}, u32[]{:S(2)}, u32[]{:S(2)}) collective-permute-start(f32[1056,128]{1,0:T(8,128)S(1)} %pad_maximum_fusion.2), channel_id=1, source_target_pairs={{0,1},{1,0},{2,3},{3,2},{4,5},{5,4},{6,7},{7,6},{8,9},{9,8},{10,11... | collective-permute-start | bytes 1622024 | tf_op jit(solution)/shard_map/ppermute | solution.py:254
  38.1 0.8 copy-start.4
  38.2 7.7 %collective-permute-start.8 = (f32[1536,128]{1,0:T(8,128)S(1)}, f32[1536,128]{1,0:T(8,128)}, u32[]{:S(2)}, u32[]{:S(2)}) collective-permute-start(f32[1536,128]{1,0:T(8,128)S(1)} %pad_maximum_fusion), channel_id=1, source_target_pairs={{0,1},{1,0},{2,3},{3,2},{4,5},{5,4},{6,7},{7,6},{8,9},{9,8},{10,11... | collective-permute-start | bytes 2359304 | tf_op jit(solution)/shard_map/ppermute | solution.py:254
  38.3 6.7 %copy-start.5 = (f32[768,128]{1,0:T(8,128)}, f32[768,128]{1,0:T(8,128)S(1)}, u32[]{:S(2)}) copy-start(f32[768,128]{1,0:T(8,128)S(1)} %collective-permute-done.10.refs_14_) | copy-start | bytes 1179652
  38.9 7.0 %collective-permute-start.11 = (f32[1536,128]{1,0:T(8,128)S(1)}, f32[1536,128]{1,0:T(8,128)S(1)}, u32[]{:S(2)}, u32[]{:S(2)}) collective-permute-start(f32[1536,128]{1,0:T(8,128)S(1)} %pad_maximum_fusion.1), channel_id=1, source_target_pairs={{0,1},{1,0},{2,3},{3,2},{4,5},{5,4},{6,7},{7,6},{8,9},{9,8},{10,11... | collective-permute-start | bytes 2359304 | tf_op jit(solution)/shard_map/ppermute | solution.py:254
  38.9 0.8 copy-start.11
  39.7 0.8 copy-start.12
  45.9 0.9 %copy-start.10 = (f32[1536,128]{1,0:T(8,128)}, f32[1536,128]{1,0:T(8,128)S(1)}, u32[]{:S(2)}) copy-start(f32[1536,128]{1,0:T(8,128)S(1)} %collective-permute-done.11.refs_15_) | copy-start | bytes 2359300

commit v2 on v1

v2 whole, which is shorter than its diff:
```python
import functools

import jax
import jax.numpy as jnp
from jax import lax
from jax.experimental import pallas as pl
from jax.experimental.pallas import tpu as pltpu
from jax.sharding import PartitionSpec as P

LANES = 128
MOST = 4
SUB = 16
NTAB = 64

TIME_STEP = 0.2
EARTH_SPIN = 0.0588
J2_COEF = 0.00108263
DRAG_SCALE = 0.008
SCALE_HEIGHT = 0.1
TABLE_TOP = 0.4
SPEED_FLOOR = 0.04

F32 = jnp.float32
BF = jnp.bfloat16


def unit_rows(blocks):
    return 5 * blocks + -(-blocks // (8 * LANES)) * 8


def substep(state, ballistic, table, slopes):
    x, y, z, vx, vy, vz = state
    zz = z * z
    radius_sq = x * x + y * y + zz
    inv = lax.rsqrt(radius_sq)
    height = radius_sq * inv - 1.0
    coord = jnp.clip(height * ((NTAB - 1) / TABLE_TOP), -1.0, float(NTAB))
    cell = jnp.floor(coord)
    index = cell.astype(jnp.int32) + 1
    base = jnp.take_along_axis(table, index, axis=1, mode="promise_in_bounds")
    slope = jnp.take_along_axis(slopes, index, axis=1, mode="promise_in_bounds")
    log_density = base + (coord - cell) * slope - height * (1.0 / SCALE_HEIGHT)
    ux = vx + EARTH_SPIN * y
    uy = vy - EARTH_SPIN * x
    air_sq = ux * ux + uy * uy + vz * vz
    drag = (TIME_STEP * DRAG_SCALE) * jnp.exp(log_density) * (ballistic * jnp.sqrt(air_sq))
    inv_sq = inv * inv
    inv_cube = inv_sq * inv
    oblate = (1.5 * J2_COEF * TIME_STEP) * (inv_cube * inv_sq)
    pull = TIME_STEP * inv_cube + oblate * (1.0 - 5.0 * (zz * inv_sq))
    pull_z = pull + 2.0 * oblate
    vx = vx - x * pull - drag * ux
    vy = vy - y * pull - drag * uy
    vz = vz - z * pull_z - drag * vz
    return (x + TIME_STEP * vx, y + TIME_STEP * vy, z + TIME_STEP * vz, vx, vy, vz)


def propagate_kernel(table_ref, orbit_ref, props_ref, cube_ref, next_ref, unit_ref, tiles, props, lut, *, group, unroll):
    blocks = orbit_ref.shape[1] // LANES
    rows = group * 8
    for b in range(blocks):
        tiles[pl.ds(8 * b, 6), :] = orbit_ref[:, pl.ds(b * LANES, LANES)]
        props[pl.ds(8 * b, 3), :] = props_ref[:, pl.ds(b * LANES, LANES)]
    lut[...] = jnp.zeros((8, LANES), F32)
    lut[pl.ds(0, 1), pl.ds(0, NTAB)] = table_ref[...]
    knots = jnp.broadcast_to(lut[pl.ds(0, 1), :], (8, LANES))
    table = pltpu.roll(knots, 1, 1)
    slopes = jnp.tile(knots - table, (group, 1))
    table = jnp.tile(table, (group, 1))
    unit_ref[pl.ds(5 * blocks, unit_ref.shape[0] - 5 * blocks), :] = jnp.zeros(
        (unit_ref.shape[0] - 5 * blocks, LANES), F32
    )
    unit_ref[pl.ds(5 * blocks, blocks // LANES), :] = cube_ref[...].astype(F32)
    for i in range(blocks // rows):
        base = 8 * rows * i
        state = tuple(tiles[pl.ds(base + c, rows, stride=8), :] for c in range(6))
        radius, weight, ballistic = (props[pl.ds(base + c, rows, stride=8), :] for c in range(3))
        state = lax.fori_loop(
            0, SUB, lambda k, s: substep(s, ballistic, table, slopes), state, unroll=unroll
        )
        for c in range(6):
            tiles[pl.ds(base + c, rows, stride=8), :] = state[c]
        for c, plane in enumerate((*state[3:], radius, weight)):
            unit_ref[pl.ds(c * blocks + i * rows, rows), :] = plane
    for b in range(blocks):
        next_ref[:, pl.ds(b * LANES, LANES)] = tiles[pl.ds(8 * b, 6), :]


def propagate(density_table, orbit_state, object_props, block_cube):
    count = orbit_state.shape[1]
    blocks = count // LANES
    return pl.pallas_call(
        functools.partial(propagate_kernel, group=16, unroll=2),
        out_shape=(
            jax.ShapeDtypeStruct((6, count), F32),
            jax.ShapeDtypeStruct((unit_rows(blocks), LANES), F32),
        ),
        scratch_shapes=[
            pltpu.VMEM((blocks * 8, LANES), F32),
            pltpu.VMEM((blocks * 8, LANES), F32),
            pltpu.VMEM((8, LANES), F32),
        ],
        name="propagate",
    )(density_table.reshape(1, NTAB), orbit_state, object_props, block_cube.reshape(blocks // LANES, LANES))


def split3(a):
    high = a.astype(BF).astype(F32)
    rest = a - high
    mid = rest.astype(BF).astype(F32)
    return high, mid, rest - mid


def whole_tiles(rows):
    extra = -len(rows) % 8
    return jnp.concatenate([*rows, *([jnp.zeros((extra, LANES), F32)] if extra else [])], 0)


def partner_table(own_ids, mate_ids, most):
    none = float(len(mate_ids) * LANES)
    sub = lax.broadcasted_iota(jnp.int32, (LANES, LANES), 0).astype(F32)
    lane = lax.broadcasted_iota(jnp.int32, (LANES, LANES), 1).astype(F32)
    cols = whole_tiles(mate_ids).T
    found = []
    for own in own_ids:
        places = [
            jnp.where(cols[:, t : t + 1] == own, sub + float(t * LANES), none) for t in range(len(mate_ids))
        ]
        last = jnp.full((1, LANES), -1.0, F32)
        hits = []
        for _ in range(most):
            best = None
            for place in places:
                later = jnp.where(place > last, place, none)
                best = later if best is None else jnp.minimum(best, later)
            last = jnp.min(best, axis=0, keepdims=True)
            hits.append(last)
        found.append(hits)
    counts = [sum((hit < none).astype(F32) for hit in hits) for hits in found]
    rows = counts + [hit for hits in found for hit in hits]
    turned = whole_tiles(rows).T
    halves = len(own_ids)
    ordered = [[0.0] * (most + 2) for _ in range(halves)]
    for h in range(halves):
        count = turned[:, h : h + 1]
        ahead = 0.0
        for g in range(halves):
            before = (lane + float(g * LANES)) < (sub + float(h * LANES))
            ahead = ahead + jnp.where((counts[g] > count) | ((counts[g] == count) & before), 1.0, 0.0)
        rank = jnp.sum(ahead, axis=1, keepdims=True)
        for q in range(halves):
            here = rank == lane + float(q * LANES)
            take = lambda v: jnp.sum(jnp.where(here, v, 0.0), axis=0, keepdims=True)
            ordered[q][0] += take(sub + float(h * LANES))
            ordered[q][1] += take(count)
            for p in range(most):
                at = halves + h * most + p
                ordered[q][2 + p] += take(turned[:, at : at + 1])
    rows = [ordered[q][k] for k in range(most + 2) for q in range(halves)]
    return whole_tiles(rows).astype(jnp.int32)


def pairs_kernel(*refs, arrays, first, last, most, group):
    own_ref, *mate_refs = refs[: 1 + arrays]
    refs = refs[1 + arrays :]
    if not first:
        prev_ref, *refs = refs
    out_ref, raw, own_tiles, mate_tiles, cols, table_vmem, table, sem, table_sem = refs
    blocks = out_ref.shape[0]
    rows = unit_rows(blocks)
    halves = blocks // LANES
    copies = []
    at = 0
    for k, ref in enumerate((own_ref, *mate_refs)):
        copies.append(pltpu.make_async_copy(ref, raw.at[pl.ds(at, ref.shape[0]), :], sem.at[k]))
        at += ref.shape[0]
    for copy in copies:
        copy.start()
    units = list(range(0 if first else 1, at // rows))
    cols[...] = jnp.zeros(cols.shape, F32)
    mate_tiles[pl.ds(len(units) * blocks * 8, 8), :] = jnp.zeros((8, LANES), F32)
    for copy in copies:
        copy.wait()

    def ids(unit):
        return [raw[pl.ds(unit * rows + 5 * blocks + h, 1), :] for h in range(halves)]

    table_vmem[...] = partner_table(ids(0), [row for u in units for row in ids(u)], most)
    to_smem = pltpu.make_async_copy(table_vmem, table, table_sem.at[0])
    to_smem.start()
    one = jnp.ones((8, LANES), F32)

    def planes(unit, i):
        base = unit * rows + i * 8
        at = [pl.multiple_of(base + c * blocks, 8) for c in range(5)]
        return [raw[pl.ds(a, 8), :] for a in at]

    def own_tile(i, carry):
        vx, vy, vz, rad, _ = planes(0, i)
        speed_sq = vx * vx + vy * vy + vz * vz
        for k, row in enumerate((-2.0 * vx, -2.0 * vy, -2.0 * vz, one, speed_sq, rad * rad, 2.0 * rad, one)):
            own_tiles[pl.ds(i * 64 + k, 8, stride=8), :] = row
        return carry

    lax.fori_loop(0, blocks // 8, own_tile, 0, unroll=4)
    for n, unit in enumerate(units):

        def mate_tile(i, carry):
            vx, vy, vz, rad, wt = planes(unit, i)
            speed_sq = vx * vx + vy * vy + vz * vz + SPEED_FLOOR
            for k, row in enumerate((vx, vy, vz, speed_sq, one, wt, wt * rad, wt * rad * rad)):
                mate_tiles[pl.ds(n * blocks * 8 + i * 64 + k, 8, stride=8), :] = row
            return carry

        lax.fori_loop(0, blocks // 8, mate_tile, 0, unroll=4)
    to_smem.wait()
    lane = lax.broadcasted_iota(jnp.int32, (LANES, LANES), 1)
    is_gap = lax.broadcasted_iota(jnp.int32, (16, LANES), 0) % 8 < 5
    blank = jnp.zeros((16, LANES), BF)
    pad = jnp.zeros((80, LANES), BF)

    def stack(a, b):
        return jnp.concatenate([a, b], 0).astype(BF)

    def run(q, place, count):
        for k in range(group):
            b = table[q, place + k]
            high, mid, low = split3(own_tiles[pl.ds(pl.multiple_of(b * 8, 8), 8), :])
            lhs = jnp.concatenate([stack(high, high), stack(mid, mid), stack(high, low), pad], 0).T
            acc = None
            for p in range(count):
                mate = table[(2 + p) * halves + q, place + k]
                high, mid, low = split3(mate_tiles[pl.ds(pl.multiple_of(mate * 8, 8), 8), :])
                top, bottom = stack(high, mid), stack(low, high)
                sides = []
                for keep in (is_gap, jnp.logical_not(is_gap)):
                    upper = jnp.where(keep, top, blank)
                    sides.append(jnp.concatenate([upper, upper, jnp.where(keep, bottom, blank), pad], 0))
                both = jnp.dot(lhs, jnp.concatenate(sides, 1), preferred_element_type=F32)
                gap = jnp.maximum(both[:, :LANES], SPEED_FLOOR)
                term = both[:, LANES:] * (gap * lax.rsqrt(gap))
                acc = term if acc is None else acc + term
            total = jnp.broadcast_to(jnp.sum(acc, axis=1, keepdims=True), (LANES, LANES))
            at = pl.multiple_of(jnp.bitwise_and(b, -LANES), LANES)
            pltpu.store(cols.at[pl.ds(at, LANES), :], total, mask=lane == jnp.bitwise_and(b, LANES - 1))

    def step(g, carry):
        q = g // (LANES // group)
        place = (g % (LANES // group)) * group
        longest = table[halves + q, place]
        for count in range(1, most + 1):

            @pl.when(longest == count)
            def _():
                run(q, place, count)

        return carry

    lax.fori_loop(0, blocks // group, step, 0)
    for h in range(halves):
        at = pl.ds(h * LANES, LANES)
        total = cols[at, :].T
        rad = raw[pl.ds(3 * blocks + h * LANES, LANES), :]
        wt = raw[pl.ds(4 * blocks + h * LANES, LANES), :]
        if first:
            total = total - (4.0 * SPEED_FLOOR**0.5) * wt * rad * rad
        else:
            total = total + prev_ref[at, :]
        if last:
            total = wt * total * (1.0 / (MOST * LANES))
        out_ref[at, :] = total


def pairs(own, mates, prev, last):
    rows = own.shape[0]
    blocks = rows // 5 // LANES * LANES
    first = prev is None
    most = MOST if first else MOST - 1
    total = sum(a.shape[0] for a in (own, *mates)) // rows
    tiles = (total if first else total - 1) * blocks + 1
    table = -(-(most + 2) * (blocks // LANES) // 8) * 8
    return pl.pallas_call(
        functools.partial(pairs_kernel, arrays=len(mates), first=first, last=last, most=most, group=16),
        in_specs=[pl.BlockSpec(memory_space=pl.ANY)] * (1 + len(mates))
        + ([] if first else [pl.BlockSpec(memory_space=pltpu.VMEM)]),
        out_shape=jax.ShapeDtypeStruct((blocks, LANES), F32),
        scratch_shapes=[
            pltpu.VMEM((total * rows, LANES), F32),
            pltpu.VMEM((blocks * 8, LANES), F32),
            pltpu.VMEM((tiles * 8, LANES), F32),
            pltpu.VMEM((blocks, LANES), F32),
            pltpu.VMEM((table, LANES), jnp.int32),
            pltpu.SMEM((table, LANES), jnp.int32),
            pltpu.SemaphoreType.DMA((1 + len(mates),)),
            pltpu.SemaphoreType.DMA((1,)),
        ],
        name="pairs",
    )(own, *mates, *(() if first else (prev,)))


def exchange(own, size):
    def send(a, bit_of):
        return lax.ppermute(a, "space", [(i, i ^ bit_of(i)) for i in range(size)])

    def beside(i):
        return 1

    mate = send(own, beside)
    bits = [1 << k for k in range(1, size.bit_length() - 1)]
    if len(bits) == 2:
        def across(i):
            return bits[i % 2]

        far = send(own, across)
        far_mate = send(mate, across)
        far_beside = send(far, beside)
        corner = send(far_beside, across)
        return [[mate], [far, far_mate, far_beside, send(far_mate, beside)], [corner, send(corner, beside)]]
    held = [own, mate]
    for bit in bits:
        held.append(send(jnp.concatenate(held, 0), lambda i: bit))
    return [[mate], held[2:]]


def on_device(orbit_state, object_props, density_table, block_cube):
    next_state, own = propagate(density_table, orbit_state, object_props, block_cube)
    groups = exchange(own, lax.axis_size("space"))
    total = None
    for k, mates in enumerate(groups):
        total = pairs(own, mates, total, k == len(groups) - 1)
    return (next_state, total.reshape(orbit_state.shape[1]))


def solution(mesh):
    placed = (P(None, ("mc", "space")), P(None, ("mc", "space")), P(), P(("mc", "space")))
    return jax.shard_map(
        on_device,
        mesh=mesh,
        in_specs=placed,
        out_specs=(P(None, ("mc", "space")), P(("mc", "space"))),
        check_vma=False,
    )
```

time: 88.2 us -> 80.3 us (0.910)
  waiting for transfers between devices: 13.8 us -> 22.5 us
  local copies, waits for them, and re-layouts: 6.12 us -> 0.02 us
  other arithmetic: 5.3 us -> 0 us
  starting transfers between devices: 11.1 us -> 7.08 us
  Pallas kernels: 50.4 us -> 48.4 us
    ppermute x12 -> x7, waiting for transfers between devices: 13.8 us -> 22.5 us  [send(): return lax.ppermute(a, 'space', [(i, i ^ bit_of(i)) for i in range(size)])]
    unnamed x42 -> x10, local copies, waits for them, and re-layouts: 4.46 us -> 0.02 us
    ppermute x12 -> x7, starting transfers between devices: 11.1 us -> 7.08 us  [send(): return lax.ppermute(a, 'space', [(i, i ^ bit_of(i)) for i in range(size)])]
    reduce_min x4 -> x0, other arithmetic: 2.47 us -> none  [find_partners(): jnp.min(jnp.where(same & (index > last[:, None]), index, total), axis=1)]
    pallas_call x1 -> x3, Pallas kernels: 40.9 us -> 38.7 us  [pairs(): pl.pallas_call(functools.partial(pairs_kernel, arrays=len(mates), first=f...]
    reduce_sum x4 -> x0, other arithmetic: 1.16 us -> none  [the longest x1 0.73 us: find_partners(): most = jnp.sum(at_slot * count[None, :], axis=1)[::group]]
  transfers between devices with their start and end apart: 12 -> 7, of which waited for: 4 -> 3; matrix products, arithmetic and copies ran while one was open for 7% -> 0% of each run, Pallas kernels for 11% -> 37%
where the time goes in v2:
time: 80.3 us; the launch traced here: 78.9 us
  Pallas kernels  48.4 us (60%)
  waiting for transfers between devices  22.5 us (28%)
  starting transfers between devices  7.08 us (9%)
  between operations  0.88 us (1%)
    pallas_call x3, Pallas kernels, pairs(): pl.pallas_call(functools.partial(pairs_kernel, arrays=len(mates), first=f...  38.7 us
    ppermute x7, waiting for transfers between devices, send(): return lax.ppermute(a, 'space', [(i, i ^ bit_of(i)) for i in range(size)])  22.5 us
    pallas_call x1, Pallas kernels, propagate(): pl.pallas_call(functools.partial(propagate_kernel, group=16, unroll=2), o...  9.75 us
    ppermute x7, starting transfers between devices, send(): return lax.ppermute(a, 'space', [(i, i ^ bit_of(i)) for i in range(size)])  7.08 us
  transfers between devices with their start and end apart: 7, of which 3 were waited for; matrix products, arithmetic and copies ran while one was open for 0% of the time, Pallas kernels for 37%

profile of v2, /device:TPU:0, one launch (start us, length us, event | category | flops | bytes accessed | tf_op | source)
XLA Modules:
  0.0 78.9 jit_solution(16463700292099801401)
XLA Ops:
  0.6 9.7 %propagate.1 = (f32[6,32768]{1,0:T(8,128)}, f32[1288,128]{1,0:T(8,128)}) custom-call(f32[1,64]{1,0:T(1,128)} %bitcast.5, f32[6,32768]{1,0:T(8,128)} %orbit_ref.1, f32[3,32768]{1,0:T(4,128)} %props_ref.1, s32[2,128]{1,0:T(2,128)} %bitcast.4), custom_call_target="tpu_custom_call" | custom-call | tf_op jit(solution)/shard_map/propagate/pallas_call | solution.py:92
  10.4 3.0 %collective-permute-start = (f32[1288,128]{1,0:T(8,128)}, f32[1288,128]{1,0:T(8,128)S(1)}, u32[]{:S(2)}, u32[]{:S(2)}) collective-permute-start(f32[1288,128]{1,0:T(8,128)} %get-tuple-element.5.refs_0_), channel_id=1, source_target_pairs={{0,2},{1,5},{2,0},{3,7},{4,6},{5,1},{6,4},{7,3},{8,10},{9,13},{10,... | collective-permute-start | bytes 1978376 | tf_op jit(solution)/shard_map/ppermute | solution.py:303
  13.3 0.0 collective-permute-start.4
  13.3 8.8 %collective-permute-done.refs_1_ = f32[1288,128]{1,0:T(8,128)S(1)} collective-permute-done((f32[1288,128]{1,0:T(8,128)}, f32[1288,128]{1,0:T(8,128)S(1)}, u32[]{:S(2)}, u32[]{:S(2)}) %collective-permute-start) | collective-permute-done | bytes 659488 | tf_op jit(solution)/shard_map/ppermute | solution.py:303
  22.2 0.0 copy-start
  22.2 0.0 collective-permute-start.1
  22.2 0.0 collective-permute-done.4.refs_1_
  22.2 0.0 copy-start.1
  22.2 2.1 %collective-permute-start.5 = (f32[1288,128]{1,0:T(8,128)S(1)}, f32[1288,128]{1,0:T(8,128)S(1)}, u32[]{:S(2)}, u32[]{:S(2)}) collective-permute-start(f32[1288,128]{1,0:T(8,128)S(1)} %collective-permute-done.4.refs_1_), channel_id=1, source_target_pairs={{0,2},{1,5},{2,0},{3,7},{4,6},{5,1},{6,4},{7,3},{8,10},{9,13},{10,... | collective-permute-start | bytes 1978376 | tf_op jit(solution)/shard_map/ppermute | solution.py:303
  24.3 0.0 collective-permute-done.1.refs_3_
  24.3 0.0 copy-start.2
  24.3 2.0 %collective-permute-start.2 = (f32[1288,128]{1,0:T(8,128)S(1)}, f32[1288,128]{1,0:T(8,128)S(1)}, u32[]{:S(2)}, u32[]{:S(2)}) collective-permute-start(f32[1288,128]{1,0:T(8,128)S(1)} %collective-permute-done.1.refs_3_), channel_id=1, source_target_pairs={{0,2},{1,5},{2,0},{3,7},{4,6},{5,1},{6,4},{7,3},{8,10},{9,13},{10,... | collective-permute-start | bytes 1978376 | tf_op jit(solution)/shard_map/ppermute | solution.py:303
  26.3 6.6 %collective-permute-done.5.refs_2_ = f32[1288,128]{1,0:T(8,128)S(1)} collective-permute-done((f32[1288,128]{1,0:T(8,128)S(1)}, f32[1288,128]{1,0:T(8,128)S(1)}, u32[]{:S(2)}, u32[]{:S(2)}) %collective-permute-start.5) | collective-permute-done | bytes 659488 | tf_op jit(solution)/shard_map/ppermute | solution.py:303
  32.9 0.0 copy-start.4
  32.9 0.0 collective-permute-start.6
  32.9 7.1 %collective-permute-done.2.refs_1_ = f32[1288,128]{1,0:T(8,128)S(1)} collective-permute-done((f32[1288,128]{1,0:T(8,128)S(1)}, f32[1288,128]{1,0:T(8,128)S(1)}, u32[]{:S(2)}, u32[]{:S(2)}) %collective-permute-start.2) | collective-permute-done | bytes 659488 | tf_op jit(solution)/shard_map/ppermute | solution.py:303
  39.9 0.0 copy-start.3
  40.0 0.0 collective-permute-start.3
  40.0 0.0 copy-done.1
  40.0 15.8 %pairs.3.refs_5_ = f32[256,128]{1,0:T(8,128)} custom-call(f32[1288,128]{1,0:T(8,128)} %get-tuple-element.5.refs_0_, f32[1288,128]{1,0:T(8,128)} %copy-done.1), custom_call_target="tpu_custom_call" | custom-call | tf_op jit(solution)/shard_map/pairs/pallas_call | solution.py:282
  55.8 0.0 copy-done
  55.8 0.0 copy-done.2
  55.8 0.0 collective-permute-done.6.refs_4_
  55.8 0.0 copy-done.4
  55.8 13.4 %pairs.4.refs_3_ = f32[256,128]{1,0:T(8,128)} custom-call(f32[1288,128]{1,0:T(8,128)} %get-tuple-element.5.refs_0_, f32[1288,128]{1,0:T(8,128)} %copy-done, f32[1288,128]{1,0:T(8,128)} %copy-done.4, f32[1288,128]{1,0:T(8,128)} %copy-done.2, f32[1288,128]{1,0:T(8,128)} %collective-permute-done.6.refs_4_, f32[256,128]{1,0:T(8,128)} %pairs.3.refs_5_), custom_call_target="tpu_custom_call" | custom-call | tf_op jit(solution)/shard_map/pairs/pallas_call | solution.py:282
  69.2 0.0 copy-done.3
  69.2 0.0 collective-permute-done.3.refs_2_
  69.2 9.5 %pairs.5 = f32[256,128]{1,0:T(8,128)} custom-call(f32[1288,128]{1,0:T(8,128)} %get-tuple-element.5.refs_0_, f32[1288,128]{1,0:T(8,128)} %copy-done.3, f32[1288,128]{1,0:T(8,128)} %collective-permute-done.3.refs_2_, f32[256,128]{1,0:T(8,128)} %pairs.4.refs_3_), custom_call_target="tpu_custom_call" | custom-call | tf_op jit(solution)/shard_map/pairs/pallas_call | solution.py:282
Async XLA Ops:
  10.4 11.8 %collective-permute-start = (f32[1288,128]{1,0:T(8,128)}, f32[1288,128]{1,0:T(8,128)S(1)}, u32[]{:S(2)}, u32[]{:S(2)}) collective-permute-start(f32[1288,128]{1,0:T(8,128)} %get-tuple-element.5.refs_0_), channel_id=1, source_target_pairs={{0,2},{1,5},{2,0},{3,7},{4,6},{5,1},{6,4},{7,3},{8,10},{9,13},{10,... | collective-permute-start | bytes 1978376 | tf_op jit(solution)/shard_map/ppermute | solution.py:303
  13.3 8.8 %collective-permute-start.4 = (f32[1288,128]{1,0:T(8,128)}, f32[1288,128]{1,0:T(8,128)S(1)}, u32[]{:S(2)}, u32[]{:S(2)}) collective-permute-start(f32[1288,128]{1,0:T(8,128)} %get-tuple-element.5.refs_0_), channel_id=1, source_target_pairs={{0,1},{1,0},{2,3},{3,2},{4,5},{5,4},{6,7},{7,6},{8,9},{9,8},{10,11... | collective-permute-start | bytes 1978376 | tf_op jit(solution)/shard_map/ppermute | solution.py:303
  22.2 33.6 %copy-start = (f32[1288,128]{1,0:T(8,128)}, f32[1288,128]{1,0:T(8,128)S(1)}, u32[]{:S(2)}) copy-start(f32[1288,128]{1,0:T(8,128)S(1)} %collective-permute-done.refs_1_) | copy-start | bytes 1978372
  22.2 2.1 %collective-permute-start.1 = (f32[1288,128]{1,0:T(8,128)S(1)}, f32[1288,128]{1,0:T(8,128)S(1)}, u32[]{:S(2)}, u32[]{:S(2)}) collective-permute-start(f32[1288,128]{1,0:T(8,128)S(1)} %collective-permute-done.refs_1_), channel_id=1, source_target_pairs={{0,1},{1,0},{2,3},{3,2},{4,5},{5,4},{6,7},{7,6},{8,9},{9,8},{10,11... | collective-permute-start | bytes 1978376 | tf_op jit(solution)/shard_map/ppermute | solution.py:303
  22.2 17.8 %copy-start.1 = (f32[1288,128]{1,0:T(8,128)}, f32[1288,128]{1,0:T(8,128)S(1)}, u32[]{:S(2)}) copy-start(f32[1288,128]{1,0:T(8,128)S(1)} %collective-permute-done.4.refs_1_) | copy-start | bytes 1978372
  22.2 10.7 %collective-permute-start.5 = (f32[1288,128]{1,0:T(8,128)S(1)}, f32[1288,128]{1,0:T(8,128)S(1)}, u32[]{:S(2)}, u32[]{:S(2)}) collective-permute-start(f32[1288,128]{1,0:T(8,128)S(1)} %collective-permute-done.4.refs_1_), channel_id=1, source_target_pairs={{0,2},{1,5},{2,0},{3,7},{4,6},{5,1},{6,4},{7,3},{8,10},{9,13},{10,... | collective-permute-start | bytes 1978376 | tf_op jit(solution)/shard_map/ppermute | solution.py:303
  24.3 31.5 %copy-start.2 = (f32[1288,128]{1,0:T(8,128)}, f32[1288,128]{1,0:T(8,128)S(1)}, u32[]{:S(2)}) copy-start(f32[1288,128]{1,0:T(8,128)S(1)} %collective-permute-done.1.refs_3_) | copy-start | bytes 1978372
  24.3 15.7 %collective-permute-start.2 = (f32[1288,128]{1,0:T(8,128)S(1)}, f32[1288,128]{1,0:T(8,128)S(1)}, u32[]{:S(2)}, u32[]{:S(2)}) collective-permute-start(f32[1288,128]{1,0:T(8,128)S(1)} %collective-permute-done.1.refs_3_), channel_id=1, source_target_pairs={{0,2},{1,5},{2,0},{3,7},{4,6},{5,1},{6,4},{7,3},{8,10},{9,13},{10,... | collective-permute-start | bytes 1978376 | tf_op jit(solution)/shard_map/ppermute | solution.py:303
  32.9 22.9 %copy-start.4 = (f32[1288,128]{1,0:T(8,128)}, f32[1288,128]{1,0:T(8,128)S(1)}, u32[]{:S(2)}) copy-start(f32[1288,128]{1,0:T(8,128)S(1)} %collective-permute-done.5.refs_2_) | copy-start | bytes 1978372
  32.9 22.9 %collective-permute-start.6 = (f32[1288,128]{1,0:T(8,128)S(1)}, f32[1288,128]{1,0:T(8,128)}, u32[]{:S(2)}, u32[]{:S(2)}) collective-permute-start(f32[1288,128]{1,0:T(8,128)S(1)} %collective-permute-done.5.refs_2_), channel_id=1, source_target_pairs={{0,1},{1,0},{2,3},{3,2},{4,5},{5,4},{6,7},{7,6},{8,9},{9,8},{10,11... | collective-permute-start | bytes 1978376 | tf_op jit(solution)/shard_map/ppermute | solution.py:303
  39.9 29.2 %copy-start.3 = (f32[1288,128]{1,0:T(8,128)}, f32[1288,128]{1,0:T(8,128)S(1)}, u32[]{:S(2)}) copy-start(f32[1288,128]{1,0:T(8,128)S(1)} %collective-permute-done.2.refs_1_) | copy-start | bytes 1978372
  40.0 29.2 %collective-permute-start.3 = (f32[1288,128]{1,0:T(8,128)S(1)}, f32[1288,128]{1,0:T(8,128)}, u32[]{:S(2)}, u32[]{:S(2)}) collective-permute-start(f32[1288,128]{1,0:T(8,128)S(1)} %collective-permute-done.2.refs_1_), channel_id=1, source_target_pairs={{0,1},{1,0},{2,3},{3,2},{4,5},{5,4},{6,7},{7,6},{8,9},{9,8},{10,11... | collective-permute-start | bytes 1978376 | tf_op jit(solution)/shard_map/ppermute | solution.py:303

commit v3 on v2

--- a/solution.py
+++ b/solution.py
@@ -104,11 +104,9 @@
     )(density_table.reshape(1, NTAB), orbit_state, object_props, block_cube.reshape(blocks // LANES, LANES))
 
 
-def split3(a):
+def split(a):
     high = a.astype(BF).astype(F32)
-    rest = a - high
-    mid = rest.astype(BF).astype(F32)
-    return high, mid, rest - mid
+    return jnp.concatenate([high, a - high], 0).astype(BF)
 
 
 def whole_tiles(rows):
@@ -116,16 +114,18 @@
     return jnp.concatenate([*rows, *([jnp.zeros((extra, LANES), F32)] if extra else [])], 0)
 
 
-def partner_table(own_ids, mate_ids, most):
+def partner_table(own_ids, mate_ids, most, own_first):
     none = float(len(mate_ids) * LANES)
     sub = lax.broadcasted_iota(jnp.int32, (LANES, LANES), 0).astype(F32)
     lane = lax.broadcasted_iota(jnp.int32, (LANES, LANES), 1).astype(F32)
     cols = whole_tiles(mate_ids).T
     found = []
-    for own in own_ids:
+    for h, own in enumerate(own_ids):
         places = [
             jnp.where(cols[:, t : t + 1] == own, sub + float(t * LANES), none) for t in range(len(mate_ids))
         ]
+        if own_first:
+            places[h] = jnp.where(sub == lane, none, places[h])
         last = jnp.full((1, LANES), -1.0, F32)
         hits = []
         for _ in range(most):
@@ -160,34 +160,46 @@
     return whole_tiles(rows).astype(jnp.int32)
 
 
-def pairs_kernel(*refs, arrays, first, last, most, group):
+def pairs_kernel(*refs, arrays, first, last, own_too, most, group):
     own_ref, *mate_refs = refs[: 1 + arrays]
     refs = refs[1 + arrays :]
     if not first:
         prev_ref, *refs = refs
-    out_ref, raw, own_tiles, mate_tiles, cols, table_vmem, table, sem, table_sem = refs
+    with_own = first or own_too
+    out_ref, raw, ids_vmem, prev_vmem, own_tiles, mate_tiles, cols, table_vmem, table, sem, ids_sem, table_sem = refs
     blocks = out_ref.shape[0]
     rows = unit_rows(blocks)
     halves = blocks // LANES
-    copies = []
+    id_rows = rows - 5 * blocks
+    copies, id_copies = [], []
     at = 0
     for k, ref in enumerate((own_ref, *mate_refs)):
         copies.append(pltpu.make_async_copy(ref, raw.at[pl.ds(at, ref.shape[0]), :], sem.at[k]))
+        for r in range(0, ref.shape[0], rows):
+            unit = (at + r) // rows
+            src = ref.at[pl.ds(r + 5 * blocks, id_rows), :]
+            dst = ids_vmem.at[pl.ds(unit * id_rows, id_rows), :]
+            id_copies.append(pltpu.make_async_copy(src, dst, ids_sem.at[unit]))
         at += ref.shape[0]
-    for copy in copies:
+    if not first:
+        copies.append(pltpu.make_async_copy(prev_ref, prev_vmem, sem.at[1 + arrays]))
+    for copy in id_copies + copies:
         copy.start()
-    units = list(range(0 if first else 1, at // rows))
+    units = list(range(0 if with_own else 1, at // rows))
     cols[...] = jnp.zeros(cols.shape, F32)
     mate_tiles[pl.ds(len(units) * blocks * 8, 8), :] = jnp.zeros((8, LANES), F32)
+    for copy in id_copies:
+        copy.wait()
+    if not first:
+
+        def ids(unit):
+            return [ids_vmem[pl.ds(unit * id_rows + h, 1), :] for h in range(halves)]
+
+        table_vmem[...] = partner_table(ids(0), [row for u in units for row in ids(u)], most, own_too)
+        to_smem = pltpu.make_async_copy(table_vmem, table, table_sem.at[0])
+        to_smem.start()
     for copy in copies:
         copy.wait()
-
-    def ids(unit):
-        return [raw[pl.ds(unit * rows + 5 * blocks + h, 1), :] for h in range(halves)]
-
-    table_vmem[...] = partner_table(ids(0), [row for u in units for row in ids(u)], most)
-    to_smem = pltpu.make_async_copy(table_vmem, table, table_sem.at[0])
-    to_smem.start()
     one = jnp.ones((8, LANES), F32)
 
     def planes(unit, i):
@@ -213,29 +225,27 @@
             return carry
 
         lax.fori_loop(0, blocks // 8, mate_tile, 0, unroll=4)
-    to_smem.wait()
+    if not first:
+        to_smem.wait()
     lane = lax.broadcasted_iota(jnp.int32, (LANES, LANES), 1)
     is_gap = lax.broadcasted_iota(jnp.int32, (16, LANES), 0) % 8 < 5
     blank = jnp.zeros((16, LANES), BF)
-    pad = jnp.zeros((80, LANES), BF)
-
-    def stack(a, b):
-        return jnp.concatenate([a, b], 0).astype(BF)
+    pad = jnp.zeros((96, LANES), BF)
 
     def run(q, place, count):
         for k in range(group):
-            b = table[q, place + k]
-            high, mid, low = split3(own_tiles[pl.ds(pl.multiple_of(b * 8, 8), 8), :])
-            lhs = jnp.concatenate([stack(high, high), stack(mid, mid), stack(high, low), pad], 0).T
+            b = q * LANES + place + k if first else table[q, place + k]
+            own = own_tiles[pl.ds(pl.multiple_of(b * 8, 8), 8), :]
+            high = own.astype(BF).astype(F32)
+            twice = [jnp.concatenate([part, part], 0).astype(BF) for part in (high, own - high)]
+            lhs = jnp.concatenate([*twice, pad], 0).T
             acc = None
             for p in range(count):
-                mate = table[(2 + p) * halves + q, place + k]
-                high, mid, low = split3(mate_tiles[pl.ds(pl.multiple_of(mate * 8, 8), 8), :])
-                top, bottom = stack(high, mid), stack(low, high)
+                mate = b if first else table[(2 + p) * halves + q, place + k]
+                parts = split(mate_tiles[pl.ds(pl.multiple_of(mate * 8, 8), 8), :])
                 sides = []
-                for keep in (is_gap, jnp.logical_not(is_gap)):
-                    upper = jnp.where(keep, top, blank)
-                    sides.append(jnp.concatenate([upper, upper, jnp.where(keep, bottom, blank), pad], 0))
+                for side in (jnp.where(is_gap, parts, blank), jnp.where(is_gap, blank, parts)):
+                    sides.append(jnp.concatenate([side, side, pad], 0))
                 both = jnp.dot(lhs, jnp.concatenate(sides, 1), preferred_element_type=F32)
                 gap = jnp.maximum(both[:, :LANES], SPEED_FLOOR)
                 term = both[:, LANES:] * (gap * lax.rsqrt(gap))
@@ -247,6 +257,9 @@
     def step(g, carry):
         q = g // (LANES // group)
         place = (g % (LANES // group)) * group
+        if first:
+            run(q, place, 1)
+            return carry
         longest = table[halves + q, place]
         for count in range(1, most + 1):
 
@@ -265,33 +278,37 @@
         if first:
             total = total - (4.0 * SPEED_FLOOR**0.5) * wt * rad * rad
         else:
-            total = total + prev_ref[at, :]
+            total = total + prev_vmem[at, :]
         if last:
             total = wt * total * (1.0 / (MOST * LANES))
         out_ref[at, :] = total
 
 
-def pairs(own, mates, prev, last):
+def pairs(own, mates, prev, own_too, last):
     rows = own.shape[0]
     blocks = rows // 5 // LANES * LANES
     first = prev is None
-    most = MOST if first else MOST - 1
+    most = MOST - 1
     total = sum(a.shape[0] for a in (own, *mates)) // rows
-    tiles = (total if first else total - 1) * blocks + 1
+    tiles = (total if first or own_too else total - 1) * blocks + 1
     table = -(-(most + 2) * (blocks // LANES) // 8) * 8
     return pl.pallas_call(
-        functools.partial(pairs_kernel, arrays=len(mates), first=first, last=last, most=most, group=16),
-        in_specs=[pl.BlockSpec(memory_space=pl.ANY)] * (1 + len(mates))
-        + ([] if first else [pl.BlockSpec(memory_space=pltpu.VMEM)]),
+        functools.partial(
+            pairs_kernel, arrays=len(mates), first=first, last=last, own_too=own_too, most=most, group=64 if first else 32
+        ),
+        in_specs=[pl.BlockSpec(memory_space=pl.ANY)] * (len(mates) + (1 if first else 2)),
         out_shape=jax.ShapeDtypeStruct((blocks, LANES), F32),
         scratch_shapes=[
             pltpu.VMEM((total * rows, LANES), F32),
+            pltpu.VMEM((total * (rows - 5 * blocks), LANES), F32),
+            pltpu.VMEM((blocks, LANES), F32),
             pltpu.VMEM((blocks * 8, LANES), F32),
             pltpu.VMEM((tiles * 8, LANES), F32),
             pltpu.VMEM((blocks, LANES), F32),
             pltpu.VMEM((table, LANES), jnp.int32),
             pltpu.SMEM((table, LANES), jnp.int32),
-            pltpu.SemaphoreType.DMA((1 + len(mates),)),
+            pltpu.SemaphoreType.DMA((2 + len(mates),)),
+            pltpu.SemaphoreType.DMA((total,)),
             pltpu.SemaphoreType.DMA((1,)),
         ],
         name="pairs",
@@ -315,7 +332,9 @@
         far_mate = send(mate, across)
         far_beside = send(far, beside)
         corner = send(far_beside, across)
-        return [[mate], [far, far_mate, far_beside, send(far_mate, beside)], [corner, send(corner, beside)]]
+        far_mate_beside = send(far_mate, beside)
+        corner_beside = send(corner, beside)
+        return [[mate, far, far_beside], [far_mate, far_mate_beside, corner, corner_beside]]
     held = [own, mate]
     for bit in bits:
         held.append(send(jnp.concatenate(held, 0), lambda i: bit))
@@ -325,9 +344,9 @@
 def on_device(orbit_state, object_props, density_table, block_cube):
     next_state, own = propagate(density_table, orbit_state, object_props, block_cube)
     groups = exchange(own, lax.axis_size("space"))
-    total = None
+    total = pairs(own, [], None, False, False)
     for k, mates in enumerate(groups):
-        total = pairs(own, mates, total, k == len(groups) - 1)
+        total = pairs(own, mates, total, k == 0, k == len(groups) - 1)
     return (next_state, total.reshape(orbit_state.shape[1]))
 
 

time: 80.3 us -> 73.2 us (0.912); the launches traced: 78.9 us -> 73 us
  Pallas kernels: 48.4 us -> 42.6 us
    pallas_call x3, Pallas kernels: 38.7 us -> 32.8 us  [pairs(): pl.pallas_call(functools.partial(pairs_kernel, arrays=len(mates), first=f...]
  transfers between devices with their start and end apart: 7 -> 7, of which waited for: 3 -> 3; matrix products, arithmetic and copies ran while one was open for 0% -> 0% of each run, Pallas kernels for 37% -> 30%
where the time goes in v3:
time: 73.2 us; the launch traced here: 73 us
  Pallas kernels  42.6 us (58%)
  waiting for transfers between devices  22.5 us (31%)
  starting transfers between devices  7.08 us (10%)
  between operations  0.88 us (1%)
    pallas_call x3, Pallas kernels, pairs(): pl.pallas_call(functools.partial(pairs_kernel, arrays=len(mates), first=f...  32.8 us
    ppermute x7, waiting for transfers between devices, send(): return lax.ppermute(a, 'space', [(i, i ^ bit_of(i)) for i in range(size)])  22.5 us
    pallas_call x1, Pallas kernels, propagate(): pl.pallas_call(functools.partial(propagate_kernel, group=16, unroll=2), o...  9.75 us
    ppermute x7, starting transfers between devices, send(): return lax.ppermute(a, 'space', [(i, i ^ bit_of(i)) for i in range(size)])  7.08 us
  transfers between devices with their start and end apart: 7, of which 3 were waited for; matrix products, arithmetic and copies ran while one was open for 0% of the time, Pallas kernels for 30%

profile of v3, /device:TPU:0, one launch (start us, length us, event | category | flops | bytes accessed | tf_op | source)
XLA Modules:
  0.0 73.0 jit_solution(16565197238582842502)
XLA Ops:
  0.6 9.7 %propagate.1 = (f32[6,32768]{1,0:T(8,128)}, f32[1288,128]{1,0:T(8,128)}) custom-call(f32[1,64]{1,0:T(1,128)} %bitcast.5, f32[6,32768]{1,0:T(8,128)} %orbit_ref.1, f32[3,32768]{1,0:T(4,128)} %props_ref.1, s32[2,128]{1,0:T(2,128)} %bitcast.4), custom_call_target="tpu_custom_call" | custom-call | tf_op jit(solution)/shard_map/propagate/pallas_call | solution.py:92
  10.4 3.0 %collective-permute-start.3 = (f32[1288,128]{1,0:T(8,128)}, f32[1288,128]{1,0:T(8,128)S(1)}, u32[]{:S(2)}, u32[]{:S(2)}) collective-permute-start(f32[1288,128]{1,0:T(8,128)} %get-tuple-element.5.refs_0_), channel_id=1, source_target_pairs={{0,2},{1,5},{2,0},{3,7},{4,6},{5,1},{6,4},{7,3},{8,10},{9,13},{10,... | collective-permute-start | bytes 1978376 | tf_op jit(solution)/shard_map/ppermute | solution.py:320
  13.3 0.0 collective-permute-start
  13.3 8.8 %collective-permute-done.3.refs_2_ = f32[1288,128]{1,0:T(8,128)S(1)} collective-permute-done((f32[1288,128]{1,0:T(8,128)}, f32[1288,128]{1,0:T(8,128)S(1)}, u32[]{:S(2)}, u32[]{:S(2)}) %collective-permute-start.3) | collective-permute-done | bytes 659488 | tf_op jit(solution)/shard_map/ppermute | solution.py:320
  22.2 0.0 copy-start
  22.2 0.0 collective-permute-start.4
  22.2 0.0 collective-permute-done.refs_1_
  22.2 0.0 copy-start.1
  22.2 2.1 %collective-permute-start.1 = (f32[1288,128]{1,0:T(8,128)S(1)}, f32[1288,128]{1,0:T(8,128)S(1)}, u32[]{:S(2)}, u32[]{:S(2)}) collective-permute-start(f32[1288,128]{1,0:T(8,128)S(1)} %collective-permute-done.refs_1_), channel_id=1, source_target_pairs={{0,2},{1,5},{2,0},{3,7},{4,6},{5,1},{6,4},{7,3},{8,10},{9,13},{10,... | collective-permute-start | bytes 1978376 | tf_op jit(solution)/shard_map/ppermute | solution.py:320
  24.3 0.0 collective-permute-done.4.refs_3_
  24.3 0.0 copy-start.3
  24.3 2.0 %collective-permute-start.5 = (f32[1288,128]{1,0:T(8,128)S(1)}, f32[1288,128]{1,0:T(8,128)S(1)}, u32[]{:S(2)}, u32[]{:S(2)}) collective-permute-start(f32[1288,128]{1,0:T(8,128)S(1)} %collective-permute-done.4.refs_3_), channel_id=1, source_target_pairs={{0,2},{1,5},{2,0},{3,7},{4,6},{5,1},{6,4},{7,3},{8,10},{9,13},{10,... | collective-permute-start | bytes 1978376 | tf_op jit(solution)/shard_map/ppermute | solution.py:320
  26.3 6.6 %collective-permute-done.1.refs_1_ = f32[1288,128]{1,0:T(8,128)S(1)} collective-permute-done((f32[1288,128]{1,0:T(8,128)S(1)}, f32[1288,128]{1,0:T(8,128)S(1)}, u32[]{:S(2)}, u32[]{:S(2)}) %collective-permute-start.1) | collective-permute-done | bytes 659488 | tf_op jit(solution)/shard_map/ppermute | solution.py:320
  32.9 0.0 copy-start.2
  32.9 0.0 collective-permute-start.2
  32.9 7.1 %collective-permute-done.5.refs_3_ = f32[1288,128]{1,0:T(8,128)S(1)} collective-permute-done((f32[1288,128]{1,0:T(8,128)S(1)}, f32[1288,128]{1,0:T(8,128)S(1)}, u32[]{:S(2)}, u32[]{:S(2)}) %collective-permute-start.5) | collective-permute-done | bytes 659488 | tf_op jit(solution)/shard_map/ppermute | solution.py:320
  39.9 0.0 copy-start.4
  40.0 0.0 collective-permute-start.6
  40.0 9.8 %pairs.3.refs_4_ = f32[256,128]{1,0:T(8,128)} custom-call(f32[1288,128]{1,0:T(8,128)} %get-tuple-element.5.refs_0_), custom_call_target="tpu_custom_call" | custom-call | tf_op jit(solution)/shard_map/pairs/pallas_call | solution.py:295
  49.7 0.0 copy-done
  49.7 0.0 copy-done.1
  49.7 0.0 copy-done.3
  49.8 11.8 %pairs.4.refs_5_ = f32[256,128]{1,0:T(8,128)} custom-call(f32[1288,128]{1,0:T(8,128)} %get-tuple-element.5.refs_0_, f32[1288,128]{1,0:T(8,128)} %copy-done.1, f32[1288,128]{1,0:T(8,128)} %copy-done, f32[1288,128]{1,0:T(8,128)} %copy-done.3, f32[256,128]{1,0:T(8,128)} %pairs.3.refs_4_), custom_call_target="tpu_custom_call" | custom-call | tf_op jit(solution)/shard_map/pairs/pallas_call | solution.py:295
  61.5 0.0 copy-done.2
  61.5 0.0 copy-done.4
  61.6 0.0 collective-permute-done.2.refs_2_
  61.6 0.0 collective-permute-done.6.refs_4_
  61.6 11.3 %pairs.5 = f32[256,128]{1,0:T(8,128)} custom-call(f32[1288,128]{1,0:T(8,128)} %get-tuple-element.5.refs_0_, f32[1288,128]{1,0:T(8,128)} %copy-done.2, f32[1288,128]{1,0:T(8,128)} %collective-permute-done.2.refs_2_, f32[1288,128]{1,0:T(8,128)} %copy-done.4, f32[1288,128]{1,0:T(8,128)} %collective-permute-done.6.refs_4_, f32[256,128]{1,0:T(8,128)} %pairs.4.refs_5_), custom_call_target="tpu_custom_call" | custom-call | tf_op jit(solution)/shard_map/pairs/pallas_call | solution.py:295
Async XLA Ops:
  10.4 11.8 %collective-permute-start.3 = (f32[1288,128]{1,0:T(8,128)}, f32[1288,128]{1,0:T(8,128)S(1)}, u32[]{:S(2)}, u32[]{:S(2)}) collective-permute-start(f32[1288,128]{1,0:T(8,128)} %get-tuple-element.5.refs_0_), channel_id=1, source_target_pairs={{0,2},{1,5},{2,0},{3,7},{4,6},{5,1},{6,4},{7,3},{8,10},{9,13},{10,... | collective-permute-start | bytes 1978376 | tf_op jit(solution)/shard_map/ppermute | solution.py:320
  13.3 8.8 %collective-permute-start = (f32[1288,128]{1,0:T(8,128)}, f32[1288,128]{1,0:T(8,128)S(1)}, u32[]{:S(2)}, u32[]{:S(2)}) collective-permute-start(f32[1288,128]{1,0:T(8,128)} %get-tuple-element.5.refs_0_), channel_id=1, source_target_pairs={{0,1},{1,0},{2,3},{3,2},{4,5},{5,4},{6,7},{7,6},{8,9},{9,8},{10,11... | collective-permute-start | bytes 1978376 | tf_op jit(solution)/shard_map/ppermute | solution.py:320
  22.2 27.6 %copy-start = (f32[1288,128]{1,0:T(8,128)}, f32[1288,128]{1,0:T(8,128)S(1)}, u32[]{:S(2)}) copy-start(f32[1288,128]{1,0:T(8,128)S(1)} %collective-permute-done.3.refs_2_) | copy-start | bytes 1978372
  22.2 2.1 %collective-permute-start.4 = (f32[1288,128]{1,0:T(8,128)S(1)}, f32[1288,128]{1,0:T(8,128)S(1)}, u32[]{:S(2)}, u32[]{:S(2)}) collective-permute-start(f32[1288,128]{1,0:T(8,128)S(1)} %collective-permute-done.3.refs_2_), channel_id=1, source_target_pairs={{0,1},{1,0},{2,3},{3,2},{4,5},{5,4},{6,7},{7,6},{8,9},{9,8},{10,11... | collective-permute-start | bytes 1978376 | tf_op jit(solution)/shard_map/ppermute | solution.py:320
  22.2 27.6 %copy-start.1 = (f32[1288,128]{1,0:T(8,128)}, f32[1288,128]{1,0:T(8,128)S(1)}, u32[]{:S(2)}) copy-start(f32[1288,128]{1,0:T(8,128)S(1)} %collective-permute-done.refs_1_) | copy-start | bytes 1978372
  22.2 10.7 %collective-permute-start.1 = (f32[1288,128]{1,0:T(8,128)S(1)}, f32[1288,128]{1,0:T(8,128)S(1)}, u32[]{:S(2)}, u32[]{:S(2)}) collective-permute-start(f32[1288,128]{1,0:T(8,128)S(1)} %collective-permute-done.refs_1_), channel_id=1, source_target_pairs={{0,2},{1,5},{2,0},{3,7},{4,6},{5,1},{6,4},{7,3},{8,10},{9,13},{10,... | collective-permute-start | bytes 1978376 | tf_op jit(solution)/shard_map/ppermute | solution.py:320
  24.3 25.5 %copy-start.3 = (f32[1288,128]{1,0:T(8,128)}, f32[1288,128]{1,0:T(8,128)S(1)}, u32[]{:S(2)}) copy-start(f32[1288,128]{1,0:T(8,128)S(1)} %collective-permute-done.4.refs_3_) | copy-start | bytes 1978372
  24.3 15.7 %collective-permute-start.5 = (f32[1288,128]{1,0:T(8,128)S(1)}, f32[1288,128]{1,0:T(8,128)S(1)}, u32[]{:S(2)}, u32[]{:S(2)}) collective-permute-start(f32[1288,128]{1,0:T(8,128)S(1)} %collective-permute-done.4.refs_3_), channel_id=1, source_target_pairs={{0,2},{1,5},{2,0},{3,7},{4,6},{5,1},{6,4},{7,3},{8,10},{9,13},{10,... | collective-permute-start | bytes 1978376 | tf_op jit(solution)/shard_map/ppermute | solution.py:320
  32.9 28.7 %copy-start.2 = (f32[1288,128]{1,0:T(8,128)}, f32[1288,128]{1,0:T(8,128)S(1)}, u32[]{:S(2)}) copy-start(f32[1288,128]{1,0:T(8,128)S(1)} %collective-permute-done.1.refs_1_) | copy-start | bytes 1978372
  32.9 28.7 %collective-permute-start.2 = (f32[1288,128]{1,0:T(8,128)S(1)}, f32[1288,128]{1,0:T(8,128)}, u32[]{:S(2)}, u32[]{:S(2)}) collective-permute-start(f32[1288,128]{1,0:T(8,128)S(1)} %collective-permute-done.1.refs_1_), channel_id=1, source_target_pairs={{0,1},{1,0},{2,3},{3,2},{4,5},{5,4},{6,7},{7,6},{8,9},{9,8},{10,11... | collective-permute-start | bytes 1978376 | tf_op jit(solution)/shard_map/ppermute | solution.py:320
  39.9 21.6 %copy-start.4 = (f32[1288,128]{1,0:T(8,128)}, f32[1288,128]{1,0:T(8,128)S(1)}, u32[]{:S(2)}) copy-start(f32[1288,128]{1,0:T(8,128)S(1)} %collective-permute-done.5.refs_3_) | copy-start | bytes 1978372
  40.0 21.6 %collective-permute-start.6 = (f32[1288,128]{1,0:T(8,128)S(1)}, f32[1288,128]{1,0:T(8,128)}, u32[]{:S(2)}, u32[]{:S(2)}) collective-permute-start(f32[1288,128]{1,0:T(8,128)S(1)} %collective-permute-done.5.refs_3_), channel_id=1, source_target_pairs={{0,1},{1,0},{2,3},{3,2},{4,5},{5,4},{6,7},{7,6},{8,9},{9,8},{10,11... | collective-permute-start | bytes 1978376 | tf_op jit(solution)/shard_map/ppermute | solution.py:320

commit v4 on v3

--- a/solution.py
+++ b/solution.py
@@ -1,4 +1,5 @@
 import functools
+import math
 
 import jax
 import jax.numpy as jnp
@@ -19,6 +20,10 @@
 SCALE_HEIGHT = 0.1
 TABLE_TOP = 0.4
 SPEED_FLOOR = 0.04
+TINY = 1e-30
+KEPT_VMEM = 8 << 20
+KERNEL_VMEM = 32 << 20
+LOG2_E = math.log2(math.e)
 
 F32 = jnp.float32
 BF = jnp.bfloat16
@@ -28,31 +33,45 @@
     return 5 * blocks + -(-blocks // (8 * LANES)) * 8
 
 
+def lookup(table, index):
+    dims = lax.GatherDimensionNumbers(
+        offset_dims=(),
+        collapsed_slice_dims=(1,),
+        start_index_map=(1,),
+        operand_batching_dims=(0,),
+        start_indices_batching_dims=(0,),
+    )
+    mode = lax.GatherScatterMode.PROMISE_IN_BOUNDS
+    return lax.gather(table, index[:, :, None], dims, (1, 1), mode=mode)
+
+
 def substep(state, ballistic, table, slopes):
-    x, y, z, vx, vy, vz = state
+    x, y, z, dx, dy, dz = state
     zz = z * z
     radius_sq = x * x + y * y + zz
     inv = lax.rsqrt(radius_sq)
-    height = radius_sq * inv - 1.0
-    coord = jnp.clip(height * ((NTAB - 1) / TABLE_TOP), -1.0, float(NTAB))
-    cell = jnp.floor(coord)
-    index = cell.astype(jnp.int32) + 1
-    base = jnp.take_along_axis(table, index, axis=1, mode="promise_in_bounds")
-    slope = jnp.take_along_axis(slopes, index, axis=1, mode="promise_in_bounds")
-    log_density = base + (coord - cell) * slope - height * (1.0 / SCALE_HEIGHT)
-    ux = vx + EARTH_SPIN * y
-    uy = vy - EARTH_SPIN * x
-    air_sq = ux * ux + uy * uy + vz * vz
-    drag = (TIME_STEP * DRAG_SCALE) * jnp.exp(log_density) * (ballistic * jnp.sqrt(air_sq))
+    radius = radius_sq * inv
+    cells = (NTAB - 1) / TABLE_TOP
+    coord = jnp.clip(radius * cells + (1.0 - cells), 0.0, NTAB + 1.0)
+    index = coord.astype(jnp.int32)
+    fraction = coord - index.astype(F32)
+    fall = LOG2_E / SCALE_HEIGHT
+    log_density = radius * -fall + (fall + math.log2(DRAG_SCALE))
+    log_density = log_density + (lookup(table, index) + fraction * lookup(slopes, index))
+    ux = dx + (TIME_STEP * EARTH_SPIN) * y
+    uy = dy - (TIME_STEP * EARTH_SPIN) * x
+    air_sq = ux * ux + uy * uy + dz * dz
+    drag = jnp.exp2(log_density) * (ballistic * (air_sq * lax.rsqrt(jnp.maximum(air_sq, TINY))))
     inv_sq = inv * inv
+    oblate = (1.5 * J2_COEF * TIME_STEP**2) * inv_sq
+    base = TIME_STEP**2 - (5.0 * oblate) * (zz * inv_sq)
     inv_cube = inv_sq * inv
-    oblate = (1.5 * J2_COEF * TIME_STEP) * (inv_cube * inv_sq)
-    pull = TIME_STEP * inv_cube + oblate * (1.0 - 5.0 * (zz * inv_sq))
-    pull_z = pull + 2.0 * oblate
-    vx = vx - x * pull - drag * ux
-    vy = vy - y * pull - drag * uy
-    vz = vz - z * pull_z - drag * vz
-    return (x + TIME_STEP * vx, y + TIME_STEP * vy, z + TIME_STEP * vz, vx, vy, vz)
+    pull = inv_cube * (base + oblate)
+    pull_z = inv_cube * (base + 3.0 * oblate)
+    dx = dx - x * pull - drag * ux
+    dy = dy - y * pull - drag * uy
+    dz = dz - z * pull_z - drag * dz
+    return (x + dx, y + dy, z + dz, dx, dy, dz)
 
 
 def propagate_kernel(table_ref, orbit_ref, props_ref, cube_ref, next_ref, unit_ref, tiles, props, lut, *, group, unroll):
@@ -62,7 +81,7 @@
         tiles[pl.ds(8 * b, 6), :] = orbit_ref[:, pl.ds(b * LANES, LANES)]
         props[pl.ds(8 * b, 3), :] = props_ref[:, pl.ds(b * LANES, LANES)]
     lut[...] = jnp.zeros((8, LANES), F32)
-    lut[pl.ds(0, 1), pl.ds(0, NTAB)] = table_ref[...]
+    lut[pl.ds(0, 1), pl.ds(0, NTAB)] = table_ref[...] * LOG2_E
     knots = jnp.broadcast_to(lut[pl.ds(0, 1), :], (8, LANES))
     table = pltpu.roll(knots, 1, 1)
     slopes = jnp.tile(knots - table, (group, 1))
@@ -73,11 +92,13 @@
     unit_ref[pl.ds(5 * blocks, blocks // LANES), :] = cube_ref[...].astype(F32)
     for i in range(blocks // rows):
         base = 8 * rows * i
-        state = tuple(tiles[pl.ds(base + c, rows, stride=8), :] for c in range(6))
+        state = [tiles[pl.ds(base + c, rows, stride=8), :] for c in range(6)]
+        state = (*state[:3], *(TIME_STEP * v for v in state[3:]))
         radius, weight, ballistic = (props[pl.ds(base + c, rows, stride=8), :] for c in range(3))
         state = lax.fori_loop(
             0, SUB, lambda k, s: substep(s, ballistic, table, slopes), state, unroll=unroll
         )
+        state = (*state[:3], *((1.0 / TIME_STEP) * d for d in state[3:]))
         for c in range(6):
             tiles[pl.ds(base + c, rows, stride=8), :] = state[c]
         for c, plane in enumerate((*state[3:], radius, weight)):
@@ -166,49 +187,31 @@
     if not first:
         prev_ref, *refs = refs
     with_own = first or own_too
-    out_ref, raw, ids_vmem, prev_vmem, own_tiles, mate_tiles, cols, table_vmem, table, sem, ids_sem, table_sem = refs
+    out_ref, own_tiles, mate_tiles, cols, table_vmem, table, table_sem = refs
     blocks = out_ref.shape[0]
     rows = unit_rows(blocks)
     halves = blocks // LANES
-    id_rows = rows - 5 * blocks
-    copies, id_copies = [], []
-    at = 0
-    for k, ref in enumerate((own_ref, *mate_refs)):
-        copies.append(pltpu.make_async_copy(ref, raw.at[pl.ds(at, ref.shape[0]), :], sem.at[k]))
-        for r in range(0, ref.shape[0], rows):
-            unit = (at + r) // rows
-            src = ref.at[pl.ds(r + 5 * blocks, id_rows), :]
-            dst = ids_vmem.at[pl.ds(unit * id_rows, id_rows), :]
-            id_copies.append(pltpu.make_async_copy(src, dst, ids_sem.at[unit]))
-        at += ref.shape[0]
+    units = [(ref, r) for ref in ((own_ref,) if with_own else ()) + tuple(mate_refs) for r in range(0, ref.shape[0], rows)]
     if not first:
-        copies.append(pltpu.make_async_copy(prev_ref, prev_vmem, sem.at[1 + arrays]))
-    for copy in id_copies + copies:
-        copy.start()
-    units = list(range(0 if with_own else 1, at // rows))
+
+        def ids(unit):
+            ref, at = unit
+            return [ref[pl.ds(at + 5 * blocks + h, 1), :] for h in range(halves)]
+
+        table_vmem[...] = partner_table(ids((own_ref, 0)), [row for u in units for row in ids(u)], most, own_too)
+        to_smem = pltpu.make_async_copy(table_vmem, table, table_sem.at[0])
+        to_smem.start()
     cols[...] = jnp.zeros(cols.shape, F32)
     mate_tiles[pl.ds(len(units) * blocks * 8, 8), :] = jnp.zeros((8, LANES), F32)
-    for copy in id_copies:
-        copy.wait()
-    if not first:
-
-        def ids(unit):
-            return [ids_vmem[pl.ds(unit * id_rows + h, 1), :] for h in range(halves)]
-
-        table_vmem[...] = partner_table(ids(0), [row for u in units for row in ids(u)], most, own_too)
-        to_smem = pltpu.make_async_copy(table_vmem, table, table_sem.at[0])
-        to_smem.start()
-    for copy in copies:
-        copy.wait()
     one = jnp.ones((8, LANES), F32)
 
     def planes(unit, i):
-        base = unit * rows + i * 8
-        at = [pl.multiple_of(base + c * blocks, 8) for c in range(5)]
-        return [raw[pl.ds(a, 8), :] for a in at]
+        ref, base = unit
+        at = [pl.multiple_of(base + c * blocks + i * 8, 8) for c in range(5)]
+        return [ref[pl.ds(a, 8), :] for a in at]
 
     def own_tile(i, carry):
-        vx, vy, vz, rad, _ = planes(0, i)
+        vx, vy, vz, rad, _ = planes((own_ref, 0), i)
         speed_sq = vx * vx + vy * vy + vz * vz
         for k, row in enumerate((-2.0 * vx, -2.0 * vy, -2.0 * vz, one, speed_sq, rad * rad, 2.0 * rad, one)):
             own_tiles[pl.ds(i * 64 + k, 8, stride=8), :] = row
@@ -273,46 +276,50 @@
     for h in range(halves):
         at = pl.ds(h * LANES, LANES)
         total = cols[at, :].T
-        rad = raw[pl.ds(3 * blocks + h * LANES, LANES), :]
-        wt = raw[pl.ds(4 * blocks + h * LANES, LANES), :]
+        rad = own_ref[pl.ds(3 * blocks + h * LANES, LANES), :]
+        wt = own_ref[pl.ds(4 * blocks + h * LANES, LANES), :]
         if first:
             total = total - (4.0 * SPEED_FLOOR**0.5) * wt * rad * rad
         else:
-            total = total + prev_vmem[at, :]
+            total = total + prev_ref[at, :]
         if last:
             total = wt * total * (1.0 / (MOST * LANES))
         out_ref[at, :] = total
 
 
-def pairs(own, mates, prev, own_too, last):
+def pairs(own, mates, prev, own_too, last, resident):
     rows = own.shape[0]
     blocks = rows // 5 // LANES * LANES
     first = prev is None
     most = MOST - 1
-    total = sum(a.shape[0] for a in (own, *mates)) // rows
-    tiles = (total if first or own_too else total - 1) * blocks + 1
+    units = sum(a.shape[0] for a in mates) // rows + (1 if first or own_too else 0)
     table = -(-(most + 2) * (blocks // LANES) // 8) * 8
+    operands = [own, *mates, *(() if first else (prev,))]
+    if resident:
+        operands = [pltpu.with_memory_space_constraint(a, pltpu.VMEM) for a in operands]
     return pl.pallas_call(
         functools.partial(
-            pairs_kernel, arrays=len(mates), first=first, last=last, own_too=own_too, most=most, group=64 if first else 32
+            pairs_kernel,
+            arrays=len(mates),
+            first=first,
+            last=last,
+            own_too=own_too,
+            most=most,
+            group=64 if first else 32,
         ),
-        in_specs=[pl.BlockSpec(memory_space=pl.ANY)] * (len(mates) + (1 if first else 2)),
+        in_specs=[pl.BlockSpec(memory_space=pltpu.VMEM)] * len(operands),
         out_shape=jax.ShapeDtypeStruct((blocks, LANES), F32),
         scratch_shapes=[
-            pltpu.VMEM((total * rows, LANES), F32),
-            pltpu.VMEM((total * (rows - 5 * blocks), LANES), F32),
-            pltpu.VMEM((blocks, LANES), F32),
             pltpu.VMEM((blocks * 8, LANES), F32),
-            pltpu.VMEM((tiles * 8, LANES), F32),
+            pltpu.VMEM(((units * blocks + 1) * 8, LANES), F32),
             pltpu.VMEM((blocks, LANES), F32),
             pltpu.VMEM((table, LANES), jnp.int32),
             pltpu.SMEM((table, LANES), jnp.int32),
-            pltpu.SemaphoreType.DMA((2 + len(mates),)),
-            pltpu.SemaphoreType.DMA((total,)),
             pltpu.SemaphoreType.DMA((1,)),
         ],
+        compiler_params=pltpu.CompilerParams(vmem_limit_bytes=KERNEL_VMEM) if resident else None,
         name="pairs",
-    )(own, *mates, *(() if first else (prev,)))
+    )(*operands)
 
 
 def exchange(own, size):
@@ -344,9 +351,10 @@
 def on_device(orbit_state, object_props, density_table, block_cube):
     next_state, own = propagate(density_table, orbit_state, object_props, block_cube)
     groups = exchange(own, lax.axis_size("space"))
-    total = pairs(own, [], None, False, False)
+    resident = sum(a.size for mates in groups for a in mates) * 4 <= KEPT_VMEM
+    total = pairs(own, [], None, False, False, resident)
     for k, mates in enumerate(groups):
-        total = pairs(own, mates, total, k == 0, k == len(groups) - 1)
+        total = pairs(own, mates, total, k == 0, k == len(groups) - 1, resident)
     return (next_state, total.reshape(orbit_state.shape[1]))
 
 

time: 73.2 us -> 67.7 us (0.925)
  Pallas kernels: 42.6 us -> 36.1 us
  local copies, waits for them, and re-layouts: 0.02 us -> 1.09 us
    pallas_call x3, Pallas kernels: 32.8 us -> 26.8 us  [pairs(): pl.pallas_call(functools.partial(pairs_kernel, arrays=len(mates), first=f...]
    unnamed x10 -> x2, local copies, waits for them, and re-layouts: 0.02 us -> 1.09 us
  transfers between devices with their start and end apart: 7 -> 7, of which waited for: 3 -> 4; matrix products, arithmetic and copies ran while one was open for 0% -> 0% of each run, Pallas kernels for 30% -> 26%
where the time goes in v4:
time: 67.7 us; the launch traced here: 67.5 us
  Pallas kernels  36.1 us (53%)
  waiting for transfers between devices  22.5 us (33%)
  starting transfers between devices  7.02 us (10%)
  local copies, waits for them, and re-layouts  1.09 us (2%)
  between operations  0.83 us (1%)
    pallas_call x3, Pallas kernels, pairs(): pl.pallas_call(functools.partial(pairs_kernel, arrays=len(mates), first=f...  26.8 us
    ppermute x7, waiting for transfers between devices, send(): return lax.ppermute(a, 'space', [(i, i ^ bit_of(i)) for i in range(size)])  22.5 us
    pallas_call x1, Pallas kernels, propagate(): pl.pallas_call(functools.partial(propagate_kernel, group=16, unroll=2), o...  9.35 us
    ppermute x7, starting transfers between devices, send(): return lax.ppermute(a, 'space', [(i, i ^ bit_of(i)) for i in range(size)])  7.02 us
  transfers between devices with their start and end apart: 7, of which 4 were waited for; matrix products, arithmetic and copies ran while one was open for 0% of the time, Pallas kernels for 26%

profile of v4, /device:TPU:0, one launch (start us, length us, event | category | flops | bytes accessed | tf_op | source)
XLA Modules:
  0.0 67.5 jit_solution(6055427158175297925)
XLA Ops:
  0.6 9.4 %propagate.1 = (f32[6,32768]{1,0:T(8,128)}, f32[1288,128]{1,0:T(8,128)}) custom-call(f32[1,64]{1,0:T(1,128)} %bitcast.5, f32[6,32768]{1,0:T(8,128)} %orbit_ref.1, f32[3,32768]{1,0:T(4,128)} %props_ref.1, s32[2,128]{1,0:T(2,128)} %bitcast.4), custom_call_target="tpu_custom_call" | custom-call | tf_op jit(solution)/shard_map/propagate/pallas_call | solution.py:113
  10.0 3.0 %collective-permute-start.3 = (f32[1288,128]{1,0:T(8,128)}, f32[1288,128]{1,0:T(8,128)S(1)}, u32[]{:S(2)}, u32[]{:S(2)}) collective-permute-start(f32[1288,128]{1,0:T(8,128)} %get-tuple-element.5.refs_0_), channel_id=1, source_target_pairs={{0,2},{1,5},{2,0},{3,7},{4,6},{5,1},{6,4},{7,3},{8,10},{9,13},{10,... | collective-permute-start | bytes 1978376 | tf_op jit(solution)/shard_map/ppermute | solution.py:327
  13.0 0.0 collective-permute-start
  13.0 8.8 %collective-permute-done.3.refs_2_ = f32[1288,128]{1,0:T(8,128)S(1)} collective-permute-done((f32[1288,128]{1,0:T(8,128)}, f32[1288,128]{1,0:T(8,128)S(1)}, u32[]{:S(2)}, u32[]{:S(2)}) %collective-permute-start.3) | collective-permute-done | bytes 659488 | tf_op jit(solution)/shard_map/ppermute | solution.py:327
  21.8 0.0 collective-permute-start.4
  21.8 0.0 collective-permute-done.refs_1_
  21.8 2.0 %collective-permute-start.1 = (f32[1288,128]{1,0:T(8,128)S(1)}, f32[1288,128]{1,0:T(8,128)S(1)}, u32[]{:S(2)}, u32[]{:S(2)}) collective-permute-start(f32[1288,128]{1,0:T(8,128)S(1)} %collective-permute-done.refs_1_), channel_id=1, source_target_pairs={{0,2},{1,5},{2,0},{3,7},{4,6},{5,1},{6,4},{7,3},{8,10},{9,13},{10,... | collective-permute-start | bytes 1978376 | tf_op jit(solution)/shard_map/ppermute | solution.py:327
  23.8 0.1 collective-permute-done.4.refs_3_
  23.9 2.0 %collective-permute-start.5 = (f32[1288,128]{1,0:T(8,128)S(1)}, f32[1288,128]{1,0:T(8,128)S(1)}, u32[]{:S(2)}, u32[]{:S(2)}) collective-permute-start(f32[1288,128]{1,0:T(8,128)S(1)} %collective-permute-done.4.refs_3_), channel_id=1, source_target_pairs={{0,2},{1,5},{2,0},{3,7},{4,6},{5,1},{6,4},{7,3},{8,10},{9,13},{10,... | collective-permute-start | bytes 1978376 | tf_op jit(solution)/shard_map/ppermute | solution.py:327
  25.9 6.5 %collective-permute-done.1.refs_1_ = f32[1288,128]{1,0:T(8,128)S(1)} collective-permute-done((f32[1288,128]{1,0:T(8,128)S(1)}, f32[1288,128]{1,0:T(8,128)S(1)}, u32[]{:S(2)}, u32[]{:S(2)}) %collective-permute-start.1) | collective-permute-done | bytes 659488 | tf_op jit(solution)/shard_map/ppermute | solution.py:327
  32.4 0.0 collective-permute-start.2
  32.4 7.1 %collective-permute-done.5.refs_3_ = f32[1288,128]{1,0:T(8,128)S(1)} collective-permute-done((f32[1288,128]{1,0:T(8,128)S(1)}, f32[1288,128]{1,0:T(8,128)S(1)}, u32[]{:S(2)}, u32[]{:S(2)}) %collective-permute-start.5) | collective-permute-done | bytes 659488 | tf_op jit(solution)/shard_map/ppermute | solution.py:327
  39.5 0.0 collective-permute-start.6
  39.5 0.0 copy-start
  39.5 1.1 %copy-done = f32[1288,128]{1,0:T(8,128)S(1)} copy-done((f32[1288,128]{1,0:T(8,128)S(1)}, f32[1288,128]{1,0:T(8,128)}, u32[]{:S(2)}) %copy-start) | copy-done | bytes 659480
  40.6 7.7 %pairs.3.refs_4_ = f32[256,128]{1,0:T(8,128)S(1)} custom-call(f32[1288,128]{1,0:T(8,128)S(1)} %copy-done), custom_call_target="tpu_custom_call" | custom-call | tf_op jit(solution)/shard_map/pairs/pallas_call | solution.py:300
  48.3 9.6 %pairs.4.refs_5_ = f32[256,128]{1,0:T(8,128)S(1)} custom-call(f32[1288,128]{1,0:T(8,128)S(1)} %copy-done, f32[1288,128]{1,0:T(8,128)S(1)} %collective-permute-done.refs_1_, f32[1288,128]{1,0:T(8,128)S(1)} %collective-permute-done.3.refs_2_, f32[1288,128]{1,0:T(8,128)S(1)} %collective-permute-done.4.refs_3_, f32[256,128]{1,0:T(8,128)S(1)} %pairs.3.refs_4_), custom_call_target="tpu_custom_call" | custom-call | tf_op jit(solution)/shard_map/pairs/pallas_call | solution.py:300
  57.9 0.0 collective-permute-done.2.refs_2_
  57.9 0.0 collective-permute-done.6.refs_4_
  57.9 9.5 %pairs.5 = f32[256,128]{1,0:T(8,128)} custom-call(f32[1288,128]{1,0:T(8,128)S(1)} %copy-done, f32[1288,128]{1,0:T(8,128)S(1)} %collective-permute-done.1.refs_1_, f32[1288,128]{1,0:T(8,128)S(1)} %collective-permute-done.2.refs_2_, f32[1288,128]{1,0:T(8,128)S(1)} %collective-permute-done.5.refs_3_, f32[1288,128]{1,0:T(8,128)S(1)} %collective-permute-done.6.refs_4_, ...), custom_call_target="tpu_custom_call" | custom-call | tf_op jit(solution)/shard_map/pairs/pallas_call | solution.py:300
Async XLA Ops:
  10.0 11.8 %collective-permute-start.3 = (f32[1288,128]{1,0:T(8,128)}, f32[1288,128]{1,0:T(8,128)S(1)}, u32[]{:S(2)}, u32[]{:S(2)}) collective-permute-start(f32[1288,128]{1,0:T(8,128)} %get-tuple-element.5.refs_0_), channel_id=1, source_target_pairs={{0,2},{1,5},{2,0},{3,7},{4,6},{5,1},{6,4},{7,3},{8,10},{9,13},{10,... | collective-permute-start | bytes 1978376 | tf_op jit(solution)/shard_map/ppermute | solution.py:327
  13.0 8.8 %collective-permute-start = (f32[1288,128]{1,0:T(8,128)}, f32[1288,128]{1,0:T(8,128)S(1)}, u32[]{:S(2)}, u32[]{:S(2)}) collective-permute-start(f32[1288,128]{1,0:T(8,128)} %get-tuple-element.5.refs_0_), channel_id=1, source_target_pairs={{0,1},{1,0},{2,3},{3,2},{4,5},{5,4},{6,7},{7,6},{8,9},{9,8},{10,11... | collective-permute-start | bytes 1978376 | tf_op jit(solution)/shard_map/ppermute | solution.py:327
  21.8 2.1 %collective-permute-start.4 = (f32[1288,128]{1,0:T(8,128)S(1)}, f32[1288,128]{1,0:T(8,128)S(1)}, u32[]{:S(2)}, u32[]{:S(2)}) collective-permute-start(f32[1288,128]{1,0:T(8,128)S(1)} %collective-permute-done.3.refs_2_), channel_id=1, source_target_pairs={{0,1},{1,0},{2,3},{3,2},{4,5},{5,4},{6,7},{7,6},{8,9},{9,8},{10,11... | collective-permute-start | bytes 1978376 | tf_op jit(solution)/shard_map/ppermute | solution.py:327
  21.8 10.6 %collective-permute-start.1 = (f32[1288,128]{1,0:T(8,128)S(1)}, f32[1288,128]{1,0:T(8,128)S(1)}, u32[]{:S(2)}, u32[]{:S(2)}) collective-permute-start(f32[1288,128]{1,0:T(8,128)S(1)} %collective-permute-done.refs_1_), channel_id=1, source_target_pairs={{0,2},{1,5},{2,0},{3,7},{4,6},{5,1},{6,4},{7,3},{8,10},{9,13},{10,... | collective-permute-start | bytes 1978376 | tf_op jit(solution)/shard_map/ppermute | solution.py:327
  23.9 15.6 %collective-permute-start.5 = (f32[1288,128]{1,0:T(8,128)S(1)}, f32[1288,128]{1,0:T(8,128)S(1)}, u32[]{:S(2)}, u32[]{:S(2)}) collective-permute-start(f32[1288,128]{1,0:T(8,128)S(1)} %collective-permute-done.4.refs_3_), channel_id=1, source_target_pairs={{0,2},{1,5},{2,0},{3,7},{4,6},{5,1},{6,4},{7,3},{8,10},{9,13},{10,... | collective-permute-start | bytes 1978376 | tf_op jit(solution)/shard_map/ppermute | solution.py:327
  32.4 25.5 %collective-permute-start.2 = (f32[1288,128]{1,0:T(8,128)S(1)}, f32[1288,128]{1,0:T(8,128)S(1)}, u32[]{:S(2)}, u32[]{:S(2)}) collective-permute-start(f32[1288,128]{1,0:T(8,128)S(1)} %collective-permute-done.1.refs_1_), channel_id=1, source_target_pairs={{0,1},{1,0},{2,3},{3,2},{4,5},{5,4},{6,7},{7,6},{8,9},{9,8},{10,11... | collective-permute-start | bytes 1978376 | tf_op jit(solution)/shard_map/ppermute | solution.py:327
  39.5 18.4 %collective-permute-start.6 = (f32[1288,128]{1,0:T(8,128)S(1)}, f32[1288,128]{1,0:T(8,128)S(1)}, u32[]{:S(2)}, u32[]{:S(2)}) collective-permute-start(f32[1288,128]{1,0:T(8,128)S(1)} %collective-permute-done.5.refs_3_), channel_id=1, source_target_pairs={{0,1},{1,0},{2,3},{3,2},{4,5},{5,4},{6,7},{7,6},{8,9},{9,8},{10,11... | collective-permute-start | bytes 1978376 | tf_op jit(solution)/shard_map/ppermute | solution.py:327
  39.5 1.1 %copy-start = (f32[1288,128]{1,0:T(8,128)S(1)}, f32[1288,128]{1,0:T(8,128)}, u32[]{:S(2)}) copy-start(f32[1288,128]{1,0:T(8,128)} %get-tuple-element.5.refs_0_) | copy-start | bytes 1978372

commit v5 on v4

--- a/solution.py
+++ b/solution.py
@@ -107,20 +107,25 @@
         next_ref[:, pl.ds(b * LANES, LANES)] = tiles[pl.ds(8 * b, 6), :]
 
 
-def propagate(density_table, orbit_state, object_props, block_cube):
+def result(shape, dtype, resident):
+    return pltpu.VMEM(shape, dtype) if resident else jax.ShapeDtypeStruct(shape, dtype)
+
+
+def propagate(density_table, orbit_state, object_props, block_cube, resident):
     count = orbit_state.shape[1]
     blocks = count // LANES
     return pl.pallas_call(
         functools.partial(propagate_kernel, group=16, unroll=2),
         out_shape=(
             jax.ShapeDtypeStruct((6, count), F32),
-            jax.ShapeDtypeStruct((unit_rows(blocks), LANES), F32),
+            result((unit_rows(blocks), LANES), F32, resident),
         ),
         scratch_shapes=[
             pltpu.VMEM((blocks * 8, LANES), F32),
             pltpu.VMEM((blocks * 8, LANES), F32),
             pltpu.VMEM((8, LANES), F32),
         ],
+        compiler_params=pltpu.CompilerParams(vmem_limit_bytes=KERNEL_VMEM) if resident else None,
         name="propagate",
     )(density_table.reshape(1, NTAB), orbit_state, object_props, block_cube.reshape(blocks // LANES, LANES))
 
@@ -184,10 +189,12 @@
 def pairs_kernel(*refs, arrays, first, last, own_too, most, group):
     own_ref, *mate_refs = refs[: 1 + arrays]
     refs = refs[1 + arrays :]
-    if not first:
-        prev_ref, *refs = refs
+    if first:
+        out_ref, lhs_ref, *refs = refs
+    else:
+        prev_ref, lhs_ref, out_ref, *refs = refs
     with_own = first or own_too
-    out_ref, own_tiles, mate_tiles, cols, table_vmem, table, table_sem = refs
+    own_tiles, mate_tiles, cols, table_vmem, table, table_sem = refs
     blocks = out_ref.shape[0]
     rows = unit_rows(blocks)
     halves = blocks // LANES
@@ -217,7 +224,8 @@
             own_tiles[pl.ds(i * 64 + k, 8, stride=8), :] = row
         return carry
 
-    lax.fori_loop(0, blocks // 8, own_tile, 0, unroll=4)
+    if first:
+        lax.fori_loop(0, blocks // 8, own_tile, 0, unroll=4)
     for n, unit in enumerate(units):
 
         def mate_tile(i, carry):
@@ -238,10 +246,15 @@
     def run(q, place, count):
         for k in range(group):
             b = q * LANES + place + k if first else table[q, place + k]
-            own = own_tiles[pl.ds(pl.multiple_of(b * 8, 8), 8), :]
-            high = own.astype(BF).astype(F32)
-            twice = [jnp.concatenate([part, part], 0).astype(BF) for part in (high, own - high)]
-            lhs = jnp.concatenate([*twice, pad], 0).T
+            features = pl.ds(pl.multiple_of(b * LANES, LANES), LANES)
+            if first:
+                own = own_tiles[pl.ds(pl.multiple_of(b * 8, 8), 8), :]
+                high = own.astype(BF).astype(F32)
+                twice = [jnp.concatenate([part, part], 0).astype(BF) for part in (high, own - high)]
+                lhs = jnp.concatenate([*twice, pad], 0).T
+                lhs_ref[features, :] = lhs
+            else:
+                lhs = lhs_ref[features, :]
             acc = None
             for p in range(count):
                 mate = b if first else table[(2 + p) * halves + q, place + k]
@@ -287,14 +300,15 @@
         out_ref[at, :] = total
 
 
-def pairs(own, mates, prev, own_too, last, resident):
+def pairs(own, mates, prev, lhs, own_too, last, resident):
     rows = own.shape[0]
     blocks = rows // 5 // LANES * LANES
     first = prev is None
     most = MOST - 1
     units = sum(a.shape[0] for a in mates) // rows + (1 if first or own_too else 0)
     table = -(-(most + 2) * (blocks // LANES) // 8) * 8
-    operands = [own, *mates, *(() if first else (prev,))]
+    operands = [own, *mates, *(() if first else (prev, lhs))]
+    total = result((blocks, LANES), F32, resident and not last)
     if resident:
         operands = [pltpu.with_memory_space_constraint(a, pltpu.VMEM) for a in operands]
     return pl.pallas_call(
@@ -308,7 +322,7 @@
             group=64 if first else 32,
         ),
         in_specs=[pl.BlockSpec(memory_space=pltpu.VMEM)] * len(operands),
-        out_shape=jax.ShapeDtypeStruct((blocks, LANES), F32),
+        out_shape=(total, result((blocks * LANES, LANES), BF, resident)) if first else total,
         scratch_shapes=[
             pltpu.VMEM((blocks * 8, LANES), F32),
             pltpu.VMEM(((units * blocks + 1) * 8, LANES), F32),
@@ -349,12 +363,14 @@
 
 
 def on_device(orbit_state, object_props, density_table, block_cube):
-    next_state, own = propagate(density_table, orbit_state, object_props, block_cube)
-    groups = exchange(own, lax.axis_size("space"))
-    resident = sum(a.size for mates in groups for a in mates) * 4 <= KEPT_VMEM
-    total = pairs(own, [], None, False, False, resident)
+    size = lax.axis_size("space")
+    blocks = block_cube.shape[0]
+    resident = size * unit_rows(blocks) * LANES * 4 <= KEPT_VMEM
+    next_state, own = propagate(density_table, orbit_state, object_props, block_cube, resident)
+    groups = exchange(own, size)
+    total, lhs = pairs(own, [], None, None, False, False, resident)
     for k, mates in enumerate(groups):
-        total = pairs(own, mates, total, k == 0, k == len(groups) - 1, resident)
+        total = pairs(own, mates, total, lhs, k == 0, k == len(groups) - 1, resident)
     return (next_state, total.reshape(orbit_state.shape[1]))
 
 

time: 67.7 us -> 67.1 us (level)
  Pallas kernels: 36.1 us -> 33.2 us
  local copies, waits for them, and re-layouts: 1.09 us -> 3.59 us
    unnamed x2 -> x8, local copies, waits for them, and re-layouts: 1.09 us -> 3.59 us
    pallas_call x1, Pallas kernels: 9.35 us -> 7.74 us  [propagate(): pl.pallas_call(functools.partial(propagate_kernel, group=16, unroll=2), o...]
    pallas_call x3, Pallas kernels: 26.8 us -> 25.4 us  [pairs(): pl.pallas_call(functools.partial(pairs_kernel, arrays=len(mates), first=f...]
  transfers between devices with their start and end apart: 7 -> 7, of which waited for: 4 -> 4; matrix products, arithmetic and copies ran while one was open for 0% -> 0% of each run, Pallas kernels for 26% -> 25%
where the time goes in v5:
time: 67.1 us; the launch traced here: 66.9 us
  Pallas kernels  33.2 us (49%)
  waiting for transfers between devices  22.3 us (33%)
  starting transfers between devices  7.03 us (10%)
  local copies, waits for them, and re-layouts  3.59 us (5%)
  between operations  0.84 us (1%)
    pallas_call x3, Pallas kernels, pairs(): pl.pallas_call(functools.partial(pairs_kernel, arrays=len(mates), first=f...  25.4 us
    ppermute x7, waiting for transfers between devices, send(): return lax.ppermute(a, 'space', [(i, i ^ bit_of(i)) for i in range(size)])  22.3 us
    pallas_call x1, Pallas kernels, propagate(): pl.pallas_call(functools.partial(propagate_kernel, group=16, unroll=2), o...  7.74 us
    ppermute x7, starting transfers between devices, send(): return lax.ppermute(a, 'space', [(i, i ^ bit_of(i)) for i in range(size)])  7.03 us
    unnamed x8, local copies, waits for them, and re-layouts  3.59 us
  transfers between devices with their start and end apart: 7, of which 4 were waited for; matrix products, arithmetic and copies ran while one was open for 0% of the time, Pallas kernels for 25%

profile of v5, /device:TPU:0, one launch (start us, length us, event | category | flops | bytes accessed | tf_op | source)
XLA Modules:
  0.0 66.9 jit_solution(15174413883888115885)
XLA Ops:
  0.6 0.0 copy-start
  0.6 1.2 %copy-done = f32[6,32768]{1,0:T(8,128)S(1)} copy-done((f32[6,32768]{1,0:T(8,128)S(1)}, f32[6,32768]{1,0:T(8,128)}, u32[]{:S(2)}) %copy-start) | copy-done | bytes 786456
  1.9 0.0 copy-start.1
  1.9 1.0 %copy-done.1 = f32[3,32768]{1,0:T(4,128)S(1)} copy-done((f32[3,32768]{1,0:T(4,128)S(1)}, f32[3,32768]{1,0:T(4,128)}, u32[]{:S(2)}) %copy-start.1) | copy-done | bytes 393240
  2.9 0.0 copy-start.2
  2.9 0.7 %copy-done.2 = s32[256]{0:T(256)S(1)} copy-done((s32[256]{0:T(256)S(1)}, s32[256]{0:T(256)}, u32[]{:S(2)}) %copy-start.2) | copy-done | bytes 1048
  3.6 0.0 copy-start.3
  3.6 0.7 copy-done.3
  4.2 7.7 %propagate.1 = (f32[6,32768]{1,0:T(8,128)}, f32[1288,128]{1,0:T(8,128)S(1)}) custom-call(f32[1,64]{1,0:T(1,128)S(1)} %bitcast.4, f32[6,32768]{1,0:T(8,128)S(1)} %copy-done, f32[3,32768]{1,0:T(4,128)S(1)} %copy-done.1, s32[2,128]{1,0:T(2,128)S(1)} %bitcast.3), custom_call_target="tpu_custom_call" | custom-call | tf_op jit(solution)/shard_map/propagate/pallas_call | solution.py:117
  12.0 3.0 %collective-permute-start.3 = (f32[1288,128]{1,0:T(8,128)S(1)}, f32[1288,128]{1,0:T(8,128)S(1)}, u32[]{:S(2)}, u32[]{:S(2)}) collective-permute-start(f32[1288,128]{1,0:T(8,128)S(1)} %get-tuple-element.7.refs_0_), channel_id=1, source_target_pairs={{0,2},{1,5},{2,0},{3,7},{4,6},{5,1},{6,4},{7,3},{8,10},{9,13},{10,... | collective-permute-start | bytes 1978376 | tf_op jit(solution)/shard_map/ppermute | solution.py:341
  14.9 0.0 collective-permute-start
  14.9 8.6 %collective-permute-done.3.refs_2_ = f32[1288,128]{1,0:T(8,128)S(1)} collective-permute-done((f32[1288,128]{1,0:T(8,128)S(1)}, f32[1288,128]{1,0:T(8,128)S(1)}, u32[]{:S(2)}, u32[]{:S(2)}) %collective-permute-start.3) | collective-permute-done | bytes 659488 | tf_op jit(solution)/shard_map/ppermute | solution.py:341
  23.6 0.0 collective-permute-start.4
  23.6 0.0 collective-permute-done.refs_1_
  23.6 2.0 %collective-permute-start.1 = (f32[1288,128]{1,0:T(8,128)S(1)}, f32[1288,128]{1,0:T(8,128)S(1)}, u32[]{:S(2)}, u32[]{:S(2)}) collective-permute-start(f32[1288,128]{1,0:T(8,128)S(1)} %collective-permute-done.refs_1_), channel_id=1, source_target_pairs={{0,2},{1,5},{2,0},{3,7},{4,6},{5,1},{6,4},{7,3},{8,10},{9,13},{10,... | collective-permute-start | bytes 1978376 | tf_op jit(solution)/shard_map/ppermute | solution.py:341
  25.6 0.1 collective-permute-done.4.refs_3_
  25.7 2.0 %collective-permute-start.5 = (f32[1288,128]{1,0:T(8,128)S(1)}, f32[1288,128]{1,0:T(8,128)S(1)}, u32[]{:S(2)}, u32[]{:S(2)}) collective-permute-start(f32[1288,128]{1,0:T(8,128)S(1)} %collective-permute-done.4.refs_3_), channel_id=1, source_target_pairs={{0,2},{1,5},{2,0},{3,7},{4,6},{5,1},{6,4},{7,3},{8,10},{9,13},{10,... | collective-permute-start | bytes 1978376 | tf_op jit(solution)/shard_map/ppermute | solution.py:341
  27.7 6.5 %collective-permute-done.1.refs_1_ = f32[1288,128]{1,0:T(8,128)S(1)} collective-permute-done((f32[1288,128]{1,0:T(8,128)S(1)}, f32[1288,128]{1,0:T(8,128)S(1)}, u32[]{:S(2)}, u32[]{:S(2)}) %collective-permute-start.1) | collective-permute-done | bytes 659488 | tf_op jit(solution)/shard_map/ppermute | solution.py:341
  34.2 0.0 collective-permute-start.2
  34.2 7.1 %collective-permute-done.5.refs_3_ = f32[1288,128]{1,0:T(8,128)S(1)} collective-permute-done((f32[1288,128]{1,0:T(8,128)S(1)}, f32[1288,128]{1,0:T(8,128)S(1)}, u32[]{:S(2)}, u32[]{:S(2)}) %collective-permute-start.5) | collective-permute-done | bytes 659488 | tf_op jit(solution)/shard_map/ppermute | solution.py:341
  41.3 0.0 collective-permute-start.6
  41.3 8.3 %pairs.3 = (f32[256,128]{1,0:T(8,128)S(1)}, bf16[32768,128]{1,0:T(8,128)(2,1)S(1)}) custom-call(f32[1288,128]{1,0:T(8,128)S(1)} %get-tuple-element.7.refs_0_), custom_call_target="tpu_custom_call" | custom-call | tf_op jit(solution)/shard_map/pairs/pallas_call | solution.py:314
  49.6 8.5 %pairs.4.refs_5_ = f32[256,128]{1,0:T(8,128)S(1)} custom-call(f32[1288,128]{1,0:T(8,128)S(1)} %get-tuple-element.7.refs_0_, f32[1288,128]{1,0:T(8,128)S(1)} %collective-permute-done.refs_1_, f32[1288,128]{1,0:T(8,128)S(1)} %collective-permute-done.3.refs_2_, f32[1288,128]{1,0:T(8,128)S(1)} %collective-permute-done.4.refs_3_, ...), custom_call_target="tpu_custom_call" | custom-call | tf_op jit(solution)/shard_map/pairs/pallas_call | solution.py:314
  58.1 0.0 collective-permute-done.2.refs_2_
  58.1 0.0 collective-permute-done.6.refs_4_
  58.1 8.6 %pairs.5 = f32[256,128]{1,0:T(8,128)} custom-call(f32[1288,128]{1,0:T(8,128)S(1)} %get-tuple-element.7.refs_0_, f32[1288,128]{1,0:T(8,128)S(1)} %collective-permute-done.1.refs_1_, f32[1288,128]{1,0:T(8,128)S(1)} %collective-permute-done.2.refs_2_, f32[1288,128]{1,0:T(8,128)S(1)} %collective-permute-done.5.refs_3_, ...), custom_call_target="tpu_custom_call" | custom-call | tf_op jit(solution)/shard_map/pairs/pallas_call | solution.py:314
Async XLA Ops:
  0.6 1.2 %copy-start = (f32[6,32768]{1,0:T(8,128)S(1)}, f32[6,32768]{1,0:T(8,128)}, u32[]{:S(2)}) copy-start(f32[6,32768]{1,0:T(8,128)} %orbit_ref.1) | copy-start | bytes 2359300
  1.9 1.0 %copy-start.1 = (f32[3,32768]{1,0:T(4,128)S(1)}, f32[3,32768]{1,0:T(4,128)}, u32[]{:S(2)}) copy-start(f32[3,32768]{1,0:T(4,128)} %props_ref.1) | copy-start | bytes 1179652
  2.9 0.7 %copy-start.2 = (s32[256]{0:T(256)S(1)}, s32[256]{0:T(256)}, u32[]{:S(2)}) copy-start(s32[256]{0:T(256)} %param.7) | copy-start | bytes 3076
  3.6 0.7 copy-start.3
  12.0 11.6 %collective-permute-start.3 = (f32[1288,128]{1,0:T(8,128)S(1)}, f32[1288,128]{1,0:T(8,128)S(1)}, u32[]{:S(2)}, u32[]{:S(2)}) collective-permute-start(f32[1288,128]{1,0:T(8,128)S(1)} %get-tuple-element.7.refs_0_), channel_id=1, source_target_pairs={{0,2},{1,5},{2,0},{3,7},{4,6},{5,1},{6,4},{7,3},{8,10},{9,13},{10,... | collective-permute-start | bytes 1978376 | tf_op jit(solution)/shard_map/ppermute | solution.py:341
  14.9 8.6 %collective-permute-start = (f32[1288,128]{1,0:T(8,128)S(1)}, f32[1288,128]{1,0:T(8,128)S(1)}, u32[]{:S(2)}, u32[]{:S(2)}) collective-permute-start(f32[1288,128]{1,0:T(8,128)S(1)} %get-tuple-element.7.refs_0_), channel_id=1, source_target_pairs={{0,1},{1,0},{2,3},{3,2},{4,5},{5,4},{6,7},{7,6},{8,9},{9,8},{10,11... | collective-permute-start | bytes 1978376 | tf_op jit(solution)/shard_map/ppermute | solution.py:341
  23.6 2.1 %collective-permute-start.4 = (f32[1288,128]{1,0:T(8,128)S(1)}, f32[1288,128]{1,0:T(8,128)S(1)}, u32[]{:S(2)}, u32[]{:S(2)}) collective-permute-start(f32[1288,128]{1,0:T(8,128)S(1)} %collective-permute-done.3.refs_2_), channel_id=1, source_target_pairs={{0,1},{1,0},{2,3},{3,2},{4,5},{5,4},{6,7},{7,6},{8,9},{9,8},{10,11... | collective-permute-start | bytes 1978376 | tf_op jit(solution)/shard_map/ppermute | solution.py:341
  23.6 10.6 %collective-permute-start.1 = (f32[1288,128]{1,0:T(8,128)S(1)}, f32[1288,128]{1,0:T(8,128)S(1)}, u32[]{:S(2)}, u32[]{:S(2)}) collective-permute-start(f32[1288,128]{1,0:T(8,128)S(1)} %collective-permute-done.refs_1_), channel_id=1, source_target_pairs={{0,2},{1,5},{2,0},{3,7},{4,6},{5,1},{6,4},{7,3},{8,10},{9,13},{10,... | collective-permute-start | bytes 1978376 | tf_op jit(solution)/shard_map/ppermute | solution.py:341
  25.7 15.6 %collective-permute-start.5 = (f32[1288,128]{1,0:T(8,128)S(1)}, f32[1288,128]{1,0:T(8,128)S(1)}, u32[]{:S(2)}, u32[]{:S(2)}) collective-permute-start(f32[1288,128]{1,0:T(8,128)S(1)} %collective-permute-done.4.refs_3_), channel_id=1, source_target_pairs={{0,2},{1,5},{2,0},{3,7},{4,6},{5,1},{6,4},{7,3},{8,10},{9,13},{10,... | collective-permute-start | bytes 1978376 | tf_op jit(solution)/shard_map/ppermute | solution.py:341
  34.2 23.9 %collective-permute-start.2 = (f32[1288,128]{1,0:T(8,128)S(1)}, f32[1288,128]{1,0:T(8,128)S(1)}, u32[]{:S(2)}, u32[]{:S(2)}) collective-permute-start(f32[1288,128]{1,0:T(8,128)S(1)} %collective-permute-done.1.refs_1_), channel_id=1, source_target_pairs={{0,1},{1,0},{2,3},{3,2},{4,5},{5,4},{6,7},{7,6},{8,9},{9,8},{10,11... | collective-permute-start | bytes 1978376 | tf_op jit(solution)/shard_map/ppermute | solution.py:341
  41.3 16.9 %collective-permute-start.6 = (f32[1288,128]{1,0:T(8,128)S(1)}, f32[1288,128]{1,0:T(8,128)S(1)}, u32[]{:S(2)}, u32[]{:S(2)}) collective-permute-start(f32[1288,128]{1,0:T(8,128)S(1)} %collective-permute-done.5.refs_3_), channel_id=1, source_target_pairs={{0,1},{1,0},{2,3},{3,2},{4,5},{5,4},{6,7},{7,6},{8,9},{9,8},{10,11... | collective-permute-start | bytes 1978376 | tf_op jit(solution)/shard_map/ppermute | solution.py:341

commit v6 on v5

--- a/solution.py
+++ b/solution.py
@@ -74,15 +74,34 @@
     return (x + dx, y + dy, z + dz, dx, dy, dz)
 
 
-def propagate_kernel(table_ref, orbit_ref, props_ref, cube_ref, next_ref, unit_ref, tiles, props, lut, *, group, unroll):
+def propagate_kernel(table_hbm, orbit_hbm, props_hbm, cube_hbm, next_hbm, unit_ref, *scratch, group, unroll):
+    table_ref, knots_ref, orbit_ref, props_ref, cube_ref, tiles, props, sem_in, sem_out = scratch
     blocks = orbit_ref.shape[1] // LANES
     rows = group * 8
-    for b in range(blocks):
-        tiles[pl.ds(8 * b, 6), :] = orbit_ref[:, pl.ds(b * LANES, LANES)]
-        props[pl.ds(8 * b, 3), :] = props_ref[:, pl.ds(b * LANES, LANES)]
-    lut[...] = jnp.zeros((8, LANES), F32)
-    lut[pl.ds(0, 1), pl.ds(0, NTAB)] = table_ref[...] * LOG2_E
-    knots = jnp.broadcast_to(lut[pl.ds(0, 1), :], (8, LANES))
+    small = [
+        pltpu.make_async_copy(table_hbm, table_ref, sem_in.at[0]),
+        pltpu.make_async_copy(cube_hbm, cube_ref, sem_in.at[1]),
+    ]
+    knots_ref[...] = jnp.zeros((8, LANES), F32)
+    for copy in small:
+        copy.start()
+    parts = range(blocks // rows)
+    arrive, leave = [], []
+    for i in parts:
+        at = pl.ds(i * rows * LANES, rows * LANES)
+        arrive.append(
+            (
+                pltpu.make_async_copy(orbit_hbm.at[:, at], orbit_ref.at[:, at], sem_in.at[2 + 2 * i]),
+                pltpu.make_async_copy(props_hbm.at[:, at], props_ref.at[:, at], sem_in.at[3 + 2 * i]),
+            )
+        )
+        leave.append(pltpu.make_async_copy(orbit_ref.at[:, at], next_hbm.at[:, at], sem_out.at[i]))
+        for copy in arrive[i]:
+            copy.start()
+    for copy in small:
+        copy.wait()
+    knots_ref[pl.ds(0, 1), pl.ds(0, NTAB)] = table_ref[...] * LOG2_E
+    knots = jnp.broadcast_to(knots_ref[pl.ds(0, 1), :], (8, LANES))
     table = pltpu.roll(knots, 1, 1)
     slopes = jnp.tile(knots - table, (group, 1))
     table = jnp.tile(table, (group, 1))
@@ -90,21 +109,31 @@
         (unit_ref.shape[0] - 5 * blocks, LANES), F32
     )
     unit_ref[pl.ds(5 * blocks, blocks // LANES), :] = cube_ref[...].astype(F32)
-    for i in range(blocks // rows):
-        base = 8 * rows * i
-        state = [tiles[pl.ds(base + c, rows, stride=8), :] for c in range(6)]
+    for i in parts:
+        for copy in arrive[i]:
+            copy.wait()
+        for b in range(rows):
+            at = pl.ds((i * rows + b) * LANES, LANES)
+            tiles[pl.ds(8 * b, 6), :] = orbit_ref[:, at]
+            props[pl.ds(8 * b, 3), :] = props_ref[:, at]
+        state = [tiles[pl.ds(c, rows, stride=8), :] for c in range(6)]
         state = (*state[:3], *(TIME_STEP * v for v in state[3:]))
-        radius, weight, ballistic = (props[pl.ds(base + c, rows, stride=8), :] for c in range(3))
+        radius, weight, ballistic = (props[pl.ds(c, rows, stride=8), :] for c in range(3))
+        unit_ref[pl.ds(3 * blocks + i * rows, rows), :] = radius
+        unit_ref[pl.ds(4 * blocks + i * rows, rows), :] = weight
         state = lax.fori_loop(
             0, SUB, lambda k, s: substep(s, ballistic, table, slopes), state, unroll=unroll
         )
         state = (*state[:3], *((1.0 / TIME_STEP) * d for d in state[3:]))
         for c in range(6):
-            tiles[pl.ds(base + c, rows, stride=8), :] = state[c]
-        for c, plane in enumerate((*state[3:], radius, weight)):
-            unit_ref[pl.ds(c * blocks + i * rows, rows), :] = plane
-    for b in range(blocks):
-        next_ref[:, pl.ds(b * LANES, LANES)] = tiles[pl.ds(8 * b, 6), :]
+            tiles[pl.ds(c, rows, stride=8), :] = state[c]
+        for c in range(3):
+            unit_ref[pl.ds(c * blocks + i * rows, rows), :] = state[3 + c]
+        for b in range(rows):
+            orbit_ref[:, pl.ds((i * rows + b) * LANES, LANES)] = tiles[pl.ds(8 * b, 6), :]
+        leave[i].start()
+    for copy in leave:
+        copy.wait()
 
 
 def result(shape, dtype, resident):
@@ -114,20 +143,32 @@
 def propagate(density_table, orbit_state, object_props, block_cube, resident):
     count = orbit_state.shape[1]
     blocks = count // LANES
+    group = 16
+    parts = blocks // (8 * group)
+    cubes = block_cube.reshape(blocks // LANES, LANES)
+    operands = (density_table.reshape(1, NTAB), orbit_state, object_props, cubes)
     return pl.pallas_call(
-        functools.partial(propagate_kernel, group=16, unroll=2),
+        functools.partial(propagate_kernel, group=group, unroll=4),
+        in_specs=[pl.BlockSpec(memory_space=pltpu.HBM)] * 4,
+        out_specs=(pl.BlockSpec(memory_space=pltpu.HBM), pl.BlockSpec(memory_space=pltpu.VMEM)),
         out_shape=(
             jax.ShapeDtypeStruct((6, count), F32),
             result((unit_rows(blocks), LANES), F32, resident),
         ),
         scratch_shapes=[
-            pltpu.VMEM((blocks * 8, LANES), F32),
-            pltpu.VMEM((blocks * 8, LANES), F32),
+            pltpu.VMEM((1, NTAB), F32),
             pltpu.VMEM((8, LANES), F32),
+            pltpu.VMEM((6, count), F32),
+            pltpu.VMEM((3, count), F32),
+            pltpu.VMEM((blocks // LANES, LANES), jnp.int32),
+            pltpu.VMEM((64 * group, LANES), F32),
+            pltpu.VMEM((64 * group, LANES), F32),
+            pltpu.SemaphoreType.DMA((2 + 2 * parts,)),
+            pltpu.SemaphoreType.DMA((parts,)),
         ],
         compiler_params=pltpu.CompilerParams(vmem_limit_bytes=KERNEL_VMEM) if resident else None,
         name="propagate",
-    )(density_table.reshape(1, NTAB), orbit_state, object_props, block_cube.reshape(blocks // LANES, LANES))
+    )(*(pltpu.with_memory_space_constraint(a, pltpu.HBM) for a in operands))
 
 
 def split(a):

time: 67.1 us -> 64.4 us (0.960)
  local copies, waits for them, and re-layouts: 3.59 us -> 0 us
  Pallas kernels: 33.2 us -> 34 us
    unnamed x8 -> x0, local copies, waits for them, and re-layouts: 3.59 us -> none
    pallas_call x1, Pallas kernels: 7.74 us -> 8.62 us  [propagate(): pl.pallas_call(functools.partial(propagate_kernel, group=group, unroll=4)...]
  transfers between devices with their start and end apart: 7 -> 7, of which waited for: 4 -> 4; matrix products, arithmetic and copies ran while one was open for 0% -> 0% of each run, Pallas kernels for 25% -> 26%
where the time goes in v6:
time: 64.4 us; the launch traced here: 64.2 us
  Pallas kernels  34 us (53%)
  waiting for transfers between devices  22.3 us (35%)
  starting transfers between devices  7.08 us (11%)
  between operations  0.84 us (1%)
    pallas_call x3, Pallas kernels, pairs(): pl.pallas_call(functools.partial(pairs_kernel, arrays=len(mates), first=f...  25.4 us
    ppermute x7, waiting for transfers between devices, send(): return lax.ppermute(a, 'space', [(i, i ^ bit_of(i)) for i in range(size)])  22.3 us
    pallas_call x1, Pallas kernels, propagate(): pl.pallas_call(functools.partial(propagate_kernel, group=group, unroll=4)...  8.62 us
    ppermute x7, starting transfers between devices, send(): return lax.ppermute(a, 'space', [(i, i ^ bit_of(i)) for i in range(size)])  7.08 us
  transfers between devices with their start and end apart: 7, of which 4 were waited for; matrix products, arithmetic and copies ran while one was open for 0% of the time, Pallas kernels for 26%

profile of v6, /device:TPU:0, one launch (start us, length us, event | category | flops | bytes accessed | tf_op | source)
XLA Modules:
  0.0 64.2 jit_solution(8845397557323453999)
XLA Ops:
  0.6 8.6 %propagate.1 = (f32[6,32768]{1,0:T(8,128)}, f32[1288,128]{1,0:T(8,128)S(1)}) custom-call(f32[1,64]{1,0:T(1,128)} %bitcast.5, f32[6,32768]{1,0:T(8,128)} %orbit_hbm.1, f32[3,32768]{1,0:T(4,128)} %props_hbm.1, s32[2,128]{1,0:T(2,128)} %bitcast.4), custom_call_target="tpu_custom_call" | custom-call | tf_op jit(solution)/shard_map/propagate/pallas_call | solution.py:150
  9.3 3.0 %collective-permute-start.3 = (f32[1288,128]{1,0:T(8,128)S(1)}, f32[1288,128]{1,0:T(8,128)S(1)}, u32[]{:S(2)}, u32[]{:S(2)}) collective-permute-start(f32[1288,128]{1,0:T(8,128)S(1)} %get-tuple-element.7.refs_0_), channel_id=1, source_target_pairs={{0,2},{1,5},{2,0},{3,7},{4,6},{5,1},{6,4},{7,3},{8,10},{9,13},{10,... | collective-permute-start | bytes 1978376 | tf_op jit(solution)/shard_map/ppermute | solution.py:382
  12.3 0.0 collective-permute-start
  12.3 8.6 %collective-permute-done.3.refs_2_ = f32[1288,128]{1,0:T(8,128)S(1)} collective-permute-done((f32[1288,128]{1,0:T(8,128)S(1)}, f32[1288,128]{1,0:T(8,128)S(1)}, u32[]{:S(2)}, u32[]{:S(2)}) %collective-permute-start.3) | collective-permute-done | bytes 659488 | tf_op jit(solution)/shard_map/ppermute | solution.py:382
  20.9 0.0 collective-permute-start.4
  20.9 0.0 collective-permute-done.refs_1_
  20.9 2.0 %collective-permute-start.1 = (f32[1288,128]{1,0:T(8,128)S(1)}, f32[1288,128]{1,0:T(8,128)S(1)}, u32[]{:S(2)}, u32[]{:S(2)}) collective-permute-start(f32[1288,128]{1,0:T(8,128)S(1)} %collective-permute-done.refs_1_), channel_id=1, source_target_pairs={{0,2},{1,5},{2,0},{3,7},{4,6},{5,1},{6,4},{7,3},{8,10},{9,13},{10,... | collective-permute-start | bytes 1978376 | tf_op jit(solution)/shard_map/ppermute | solution.py:382
  22.9 0.1 collective-permute-done.4.refs_3_
  23.0 2.0 %collective-permute-start.5 = (f32[1288,128]{1,0:T(8,128)S(1)}, f32[1288,128]{1,0:T(8,128)S(1)}, u32[]{:S(2)}, u32[]{:S(2)}) collective-permute-start(f32[1288,128]{1,0:T(8,128)S(1)} %collective-permute-done.4.refs_3_), channel_id=1, source_target_pairs={{0,2},{1,5},{2,0},{3,7},{4,6},{5,1},{6,4},{7,3},{8,10},{9,13},{10,... | collective-permute-start | bytes 1978376 | tf_op jit(solution)/shard_map/ppermute | solution.py:382
  25.0 6.5 %collective-permute-done.1.refs_1_ = f32[1288,128]{1,0:T(8,128)S(1)} collective-permute-done((f32[1288,128]{1,0:T(8,128)S(1)}, f32[1288,128]{1,0:T(8,128)S(1)}, u32[]{:S(2)}, u32[]{:S(2)}) %collective-permute-start.1) | collective-permute-done | bytes 659488 | tf_op jit(solution)/shard_map/ppermute | solution.py:382
  31.5 0.0 collective-permute-start.2
  31.5 7.1 %collective-permute-done.5.refs_3_ = f32[1288,128]{1,0:T(8,128)S(1)} collective-permute-done((f32[1288,128]{1,0:T(8,128)S(1)}, f32[1288,128]{1,0:T(8,128)S(1)}, u32[]{:S(2)}, u32[]{:S(2)}) %collective-permute-start.5) | collective-permute-done | bytes 659488 | tf_op jit(solution)/shard_map/ppermute | solution.py:382
  38.6 0.0 collective-permute-start.6
  38.6 8.3 %pairs.3 = (f32[256,128]{1,0:T(8,128)S(1)}, bf16[32768,128]{1,0:T(8,128)(2,1)S(1)}) custom-call(f32[1288,128]{1,0:T(8,128)S(1)} %get-tuple-element.7.refs_0_), custom_call_target="tpu_custom_call" | custom-call | tf_op jit(solution)/shard_map/pairs/pallas_call | solution.py:355
  46.9 8.5 %pairs.4.refs_5_ = f32[256,128]{1,0:T(8,128)S(1)} custom-call(f32[1288,128]{1,0:T(8,128)S(1)} %get-tuple-element.7.refs_0_, f32[1288,128]{1,0:T(8,128)S(1)} %collective-permute-done.refs_1_, f32[1288,128]{1,0:T(8,128)S(1)} %collective-permute-done.3.refs_2_, f32[1288,128]{1,0:T(8,128)S(1)} %collective-permute-done.4.refs_3_, ...), custom_call_target="tpu_custom_call" | custom-call | tf_op jit(solution)/shard_map/pairs/pallas_call | solution.py:355
  55.5 0.0 collective-permute-done.2.refs_2_
  55.5 0.0 collective-permute-done.6.refs_4_
  55.5 8.6 %pairs.5 = f32[256,128]{1,0:T(8,128)} custom-call(f32[1288,128]{1,0:T(8,128)S(1)} %get-tuple-element.7.refs_0_, f32[1288,128]{1,0:T(8,128)S(1)} %collective-permute-done.1.refs_1_, f32[1288,128]{1,0:T(8,128)S(1)} %collective-permute-done.2.refs_2_, f32[1288,128]{1,0:T(8,128)S(1)} %collective-permute-done.5.refs_3_, ...), custom_call_target="tpu_custom_call" | custom-call | tf_op jit(solution)/shard_map/pairs/pallas_call | solution.py:355
Async XLA Ops:
  9.3 11.6 %collective-permute-start.3 = (f32[1288,128]{1,0:T(8,128)S(1)}, f32[1288,128]{1,0:T(8,128)S(1)}, u32[]{:S(2)}, u32[]{:S(2)}) collective-permute-start(f32[1288,128]{1,0:T(8,128)S(1)} %get-tuple-element.7.refs_0_), channel_id=1, source_target_pairs={{0,2},{1,5},{2,0},{3,7},{4,6},{5,1},{6,4},{7,3},{8,10},{9,13},{10,... | collective-permute-start | bytes 1978376 | tf_op jit(solution)/shard_map/ppermute | solution.py:382
  12.3 8.6 %collective-permute-start = (f32[1288,128]{1,0:T(8,128)S(1)}, f32[1288,128]{1,0:T(8,128)S(1)}, u32[]{:S(2)}, u32[]{:S(2)}) collective-permute-start(f32[1288,128]{1,0:T(8,128)S(1)} %get-tuple-element.7.refs_0_), channel_id=1, source_target_pairs={{0,1},{1,0},{2,3},{3,2},{4,5},{5,4},{6,7},{7,6},{8,9},{9,8},{10,11... | collective-permute-start | bytes 1978376 | tf_op jit(solution)/shard_map/ppermute | solution.py:382
  20.9 2.1 %collective-permute-start.4 = (f32[1288,128]{1,0:T(8,128)S(1)}, f32[1288,128]{1,0:T(8,128)S(1)}, u32[]{:S(2)}, u32[]{:S(2)}) collective-permute-start(f32[1288,128]{1,0:T(8,128)S(1)} %collective-permute-done.3.refs_2_), channel_id=1, source_target_pairs={{0,1},{1,0},{2,3},{3,2},{4,5},{5,4},{6,7},{7,6},{8,9},{9,8},{10,11... | collective-permute-start | bytes 1978376 | tf_op jit(solution)/shard_map/ppermute | solution.py:382
  20.9 10.6 %collective-permute-start.1 = (f32[1288,128]{1,0:T(8,128)S(1)}, f32[1288,128]{1,0:T(8,128)S(1)}, u32[]{:S(2)}, u32[]{:S(2)}) collective-permute-start(f32[1288,128]{1,0:T(8,128)S(1)} %collective-permute-done.refs_1_), channel_id=1, source_target_pairs={{0,2},{1,5},{2,0},{3,7},{4,6},{5,1},{6,4},{7,3},{8,10},{9,13},{10,... | collective-permute-start | bytes 1978376 | tf_op jit(solution)/shard_map/ppermute | solution.py:382
  23.0 15.6 %collective-permute-start.5 = (f32[1288,128]{1,0:T(8,128)S(1)}, f32[1288,128]{1,0:T(8,128)S(1)}, u32[]{:S(2)}, u32[]{:S(2)}) collective-permute-start(f32[1288,128]{1,0:T(8,128)S(1)} %collective-permute-done.4.refs_3_), channel_id=1, source_target_pairs={{0,2},{1,5},{2,0},{3,7},{4,6},{5,1},{6,4},{7,3},{8,10},{9,13},{10,... | collective-permute-start | bytes 1978376 | tf_op jit(solution)/shard_map/ppermute | solution.py:382
  31.5 23.9 %collective-permute-start.2 = (f32[1288,128]{1,0:T(8,128)S(1)}, f32[1288,128]{1,0:T(8,128)S(1)}, u32[]{:S(2)}, u32[]{:S(2)}) collective-permute-start(f32[1288,128]{1,0:T(8,128)S(1)} %collective-permute-done.1.refs_1_), channel_id=1, source_target_pairs={{0,1},{1,0},{2,3},{3,2},{4,5},{5,4},{6,7},{7,6},{8,9},{9,8},{10,11... | collective-permute-start | bytes 1978376 | tf_op jit(solution)/shard_map/ppermute | solution.py:382
  38.6 16.9 %collective-permute-start.6 = (f32[1288,128]{1,0:T(8,128)S(1)}, f32[1288,128]{1,0:T(8,128)S(1)}, u32[]{:S(2)}, u32[]{:S(2)}) collective-permute-start(f32[1288,128]{1,0:T(8,128)S(1)} %collective-permute-done.5.refs_3_), channel_id=1, source_target_pairs={{0,1},{1,0},{2,3},{3,2},{4,5},{5,4},{6,7},{7,6},{8,9},{9,8},{10,11... | collective-permute-start | bytes 1978376 | tf_op jit(solution)/shard_map/ppermute | solution.py:382
